TPU v7x, 32 devices: a whole 2x2x4 slice. The times are simulated.
32 devices in a mesh: gx: 16 (over z, x, core), gy: 2 (over y).
Axes of the slice: x: 2, y: 2, z: 4, core: 2. Of those that a mesh axis runs over, the one named last changes fastest.
Arguments:
- volume_field: float32 [3, 256, 32, 128], P(None, 'gx', 'gy'), may hold values from -6 to 6
- diag_blocks: float32 [3, 3, 256, 32, 128], P(None, None, 'gx', 'gy'), may hold values from -4 to 4
- face_weights: float32 [6, 2, 256, 32, 128], P(None, None, 'gx', 'gy'), may hold values from 0.3 to 3
- boundary_field: float32 [16, 2, 1536], P('gx', 'gy'), may hold values from -6 to 6
- self_term: float32 [16, 2, 1536], P('gx', 'gy'), may hold values from 0.5 to 2
- coupling: float32 [16, 2, 1536], P('gx', 'gy'), may hold values from 0.3 to 3
- owner_map: int32 [16, 2, 1536], P('gx', 'gy'), may hold values from 0 to 1535, as said below
- left_basis: bfloat16 [32, 16, 2, 1536], P('gy', 'gx'), may hold values from -1 to 1
- right_basis: bfloat16 [256, 16, 2, 1536], P('gx', None, 'gy'), may hold values from -0.0390625 to 0.0390625
Outputs:
- volume_out: float32 [3, 256, 32, 128], P(None, 'gx', 'gy')
- boundary_out: float32 [16, 2, 1536], P('gx', 'gy')
Inputs may be any that keep to these rules, and one draw needn't show every extreme that they name: `owner_map`: within each subdomain (p, q) the 1536 entries name every surface edge of that subdomain exactly once.
All inputs are finite; a program needn't handle non-finite values.
Results may differ from a plain program's by a relative error of at most 0.0017.
Values may be sent and summed in bfloat16 or wider, within the bound.
No kernel may reach another device: no remote copies, remote signals or barrier semaphores. Data moves between devices by JAX's collectives and lax.ppermute only.
A program may use at most 64 MiB of HBM per device.

v0:
```python
import jax
import jax.numpy as jnp
from jax import lax
from jax.sharding import PartitionSpec as P


def with_halo(value, sides, width):
    for axis, dim in sides:
        devices, length = (lax.axis_size(axis), value.shape[dim])
        up = [(i, (i + 1) % devices) for i in range(devices - 1)]
        down = [(j, i) for i, j in up]
        last = lax.slice_in_dim(value, length - width, length, axis=dim)
        initial = lax.slice_in_dim(value, 0, width, axis=dim)
        before = lax.ppermute(last, axis, up)
        after = lax.ppermute(initial, axis, down)
        value = jnp.concatenate([before, value, after], axis=dim)
    return value


def apply_blocks(field_in, diag_blocks, face_weights, neighbours):
    comp_rows = []
    for comp in range(3):
        accum_row = (
            diag_blocks[comp, 0] * field_in[0]
            + diag_blocks[comp, 1] * field_in[1]
            + diag_blocks[comp, 2] * field_in[2]
        )
        comp_rows.append(accum_row)
    for offset in range(6):
        direction = offset // 2
        tangent = [comp for comp in range(3) if comp != direction]
        for slot in range(2):
            comp_rows[tangent[slot]] = (
                comp_rows[tangent[slot]] - face_weights[offset, slot] * neighbours[offset][slot]
            )
    return jnp.stack(comp_rows)


def on_device(
    volume_field,
    diag_blocks,
    face_weights,
    boundary_field,
    self_term,
    coupling,
    owner_map,
    left_basis,
    right_basis,
):
    z_padded = jnp.pad(volume_field[0:2], ((0, 0), (0, 0), (0, 0), (1, 1)))
    plus_z = z_padded[..., 2:]
    minus_z = z_padded[..., :-2]
    padded = with_halo(volume_field, (("gx", 1), ("gy", 2)), 1)
    plus_x = padded[1:3, 2:, 1:-1]
    minus_x = padded[1:3, :-2, 1:-1]
    plus_y = padded[0::2, 1:-1, 2:]
    minus_y = padded[0::2, 1:-1, :-2]
    neighbours = [plus_x, minus_x, plus_y, minus_y, plus_z, minus_z]
    stiffness = apply_blocks(volume_field, diag_blocks, face_weights, neighbours)
    cells_x = volume_field.shape[1]
    cells_y = volume_field.shape[2]
    boundary_count = boundary_field.shape[2]
    surface = jnp.stack([volume_field[..., 0], volume_field[..., -1]]).reshape(boundary_count)
    owner_flat = owner_map.reshape(boundary_count)
    edge_trace = surface[owner_flat].reshape(boundary_field.shape)
    placed = (
        jnp.zeros((boundary_count,), jnp.float32)
        .at[owner_flat]
        .set((coupling * boundary_field).reshape(boundary_count))
    )
    placed = placed.reshape(2, 3, cells_x, cells_y)
    volume_out = stiffness.at[:, :, :, 0].add(placed[0]).at[:, :, :, -1].add(placed[1])
    boundary_half = boundary_field.astype(jnp.bfloat16)
    gathered = lax.all_gather(boundary_half, "gx", axis=0, tiled=True)
    coef = jnp.einsum("rxbk,xbk->r", right_basis, gathered, preferred_element_type=jnp.float32)
    coef_half = coef.astype(jnp.bfloat16)
    partial_value = jnp.einsum(
        "rabk,r->abk", left_basis, coef_half, preferred_element_type=jnp.float32
    )
    integral = lax.psum_scatter(partial_value, "gy", scatter_dimension=1, tiled=True)
    boundary_out = self_term * boundary_field + integral + coupling * edge_trace
    return (volume_out, boundary_out)


def solution(mesh):
    return jax.shard_map(
        on_device,
        mesh=mesh,
        in_specs=(
            P(None, "gx", "gy", None),
            P(None, None, "gx", "gy", None),
            P(None, None, "gx", "gy", None),
            P("gx", "gy", None),
            P("gx", "gy", None),
            P("gx", "gy", None),
            P("gx", "gy", None),
            P("gy", "gx", None, None),
            P("gx", None, "gy", None),
        ),
        out_specs=(P(None, "gx", "gy", None), P("gx", "gy", None)),
        check_vma=False,
    )
```

profile of v0, /device:TPU:0, one launch (start us, length us, event | category | flops | bytes accessed | tf_op | source)
XLA Modules:
  0.0 75.5 jit_solution(9150187020478586098)
XLA Ops:
  0.6 0.0 copy-start
  0.6 0.0 copy-start.5
  0.7 0.0 copy-start.4
  0.7 0.0 copy-start.8
  0.7 1.4 %fusion.40 = (f32[3,1,16,128]{3,2,1,0:T(8,128)}, f32[3,1,16,128]{3,2,1,0:T(8,128)}) fusion(f32[3,16,16,128]{3,2,1,0:T(8,128)} %param.13), kind=kLoop, calls=%fused_computation.77 | loop fusion | bytes 98304 | tf_op jit(solution)/shard_map/slice | solution.py:13
  2.1 3.0 %collective-permute-start = (f32[3,1,16,128]{3,2,1,0:T(8,128)}, f32[3,1,16,128]{3,2,1,0:T(8,128)}, u32[]{:S(2)}, u32[]{:S(2)}) collective-permute-start(f32[3,1,16,128]{3,2,1,0:T(8,128)} %get-tuple-element.42), channel_id=1, source_target_pairs={{0,2},{2,4},{4,6},{6,8},{8,10},{10,12},{12,14},{14,16},{16,18},{18... | collective-permute-start | bytes 73736 | tf_op jit(solution)/shard_map/ppermute | solution.py:14
  5.1 1.3 %collective-permute-start.1 = (f32[3,1,16,128]{3,2,1,0:T(8,128)}, f32[3,1,16,128]{3,2,1,0:T(8,128)}, u32[]{:S(2)}, u32[]{:S(2)}) collective-permute-start(f32[3,1,16,128]{3,2,1,0:T(8,128)} %get-tuple-element.41), channel_id=1, source_target_pairs={{2,0},{4,2},{6,4},{8,6},{10,8},{12,10},{14,12},{16,14},{18,16},{20... | collective-permute-start | bytes 73736 | tf_op jit(solution)/shard_map/ppermute | solution.py:15
  6.4 1.3 %fusion.39 = (f32[3,16,16,1]{3,2,1,0:T(8,128)S(1)}, f32[3,16,16,1]{3,2,1,0:T(8,128)S(1)}) fusion(f32[3,16,16,128]{3,2,1,0:T(8,128)} %param.13), kind=kLoop, calls=%fused_computation.76 | loop fusion | bytes 12288 | tf_op jit(solution)/shard_map/slice | solution.py:63
  7.7 0.3 copy.61
  8.0 0.4 copy.62
  8.4 0.1 reshape.175
  8.5 0.0 copy-done.5
  8.6 0.0 copy-done.4
  8.6 24.6 %all_gather.3 = bf16[16,1,1536]{2,1,0:T(2,128)(2,1)S(1)} all-gather(bf16[1,1,1536]{2,1,0:T(2,128)(2,1)S(1)} %convert_element_type.8), channel_id=1, replica_groups=mesh['gx'=16,'gy'=2] {'gx'}, dimensions={0}, use_global_device_ids=true | all-gather | bytes 52224 | tf_op jit(solution)/shard_map/all_gather | solution.py:74
  33.2 0.0 copy-done
  33.2 0.0 copy-done.8
  33.2 1.1 %fusion.4 = f32[1,2,1536]{2,0,1:T(1,128)S(1)} fusion(bf16[16,16,1536]{2,1,0:T(8,128)(2,1)S(1)} %bitcast.103, bf16[16,1,1536]{2,1,0:T(2,128)(2,1)S(1)} %all_gather.3, bf16[16,2,1536]{2,1,0:T(2,128)(2,1)S(1)} %bitcast.100), kind=kOutput, calls=%fused_computation.10 | convolution fusion | flops 884752 | bytes 946176 | tf_op jit(solution)/shard_map/rabk,r->abk/dot_general | solution.py:77
  34.4 8.1 %all-reduce.1 = f32[1,2,1536]{2,1,0:T(2,128)S(1)} all-reduce(f32[1,2,1536]{2,1,0:T(2,128)S(1)} %copy.58), channel_id=2, replica_groups=mesh['gx'=16,'gy'=2] {'gy'}, use_global_device_ids=true, to_apply=%region_1.2.clone | all-reduce | flops 3072 | bytes 24576
  42.5 0.0 copy-start.1
  42.5 0.0 copy-start.3
  42.5 8.4 %gather_fusion = f32[1536]{0:T(1024)S(1)} fusion(f32[1536]{0:T(1024)S(1)} %reshape.175, s32[2048]{0:T(1024)S(1)} %pad_clamp_fusion), kind=kCustom, calls=%fused_computation | custom fusion | bytes 18432 | tf_op jit(solution)/shard_map/gather | solution.py:65
  50.9 0.0 copy-start.2
  50.9 0.0 copy-done.9
  50.9 0.7 dynamic-slice.14
  51.6 0.0 copy-done.6
  51.6 0.0 copy-done.7
  51.6 1.3 %fusion.34 = (f32[1,1,1536]{2,1,0:T(1,128)}, f32[1536]{0:T(1024)S(1)}) fusion(f32[1,2,1536]{2,1,0:T(2,128)S(1)} %all-reduce.1, u32[]{:T(128)} %bitcast.32, f32[1,1,1536]{2,1,0:T(1,128)S(1)} %copy-done.6, f32[1536]{0:T(1024)S(1)} %gather_fusion, f32[1,1,1536]{2,1,0:T(1,128)S(1)} %copy-done.7, f32[1,1,1536]{2,1,0:T(1,128)S(1)} %copy-done.4), kind=kLoop, calls=%fused_computation.70 | loop fusion | flops 7680 | bytes 43012 | tf_op jit(solution)/shard_map/add | solution.py:81
  52.9 6.2 %scatter_custom_fusion = f32[1536]{0:T(1024)S(1)} fusion(s32[1536]{0:T(1024)S(1)} %fusion.33, f32[1536]{0:T(1024)S(1)} %get-tuple-element.48, f32[]{:T(128)} %constant.58.clone.1), kind=kCustom, calls=%fused_computation.72 | custom fusion | bytes 6148 | tf_op jit(solution)/shard_map/scatter | solution.py:69
  59.1 0.6 fusion.41
  59.7 0.0 copy-done.1
  59.7 0.1 reshape.170
  59.8 0.8 reshape.171
  60.5 0.0 collective-permute-done
  60.5 0.7 constant_dynamic-update-slice_fusion.6
  61.3 0.1 constant_dynamic-update-slice_fusion.4
  61.4 0.0 collective-permute-done.1
  61.4 0.7 constant_dynamic-update-slice_fusion.3
  62.2 2.4 %collective-permute-start.2 = (f32[3,18,1,128]{3,2,1,0:T(1,128)S(1)}, f32[3,18,1,128]{3,2,1,0:T(1,128)S(1)}, u32[]{:S(2)}, u32[]{:S(2)}) collective-permute-start(f32[3,18,1,128]{3,2,1,0:T(1,128)S(1)} %get-tuple-element.34), channel_id=1, source_target_pairs={{0,1},{2,3},{4,5},{6,7},{8,9},{10,11},{12,13},{14,15},{16,17},{18,... | collective-permute-start | bytes 82952 | tf_op jit(solution)/shard_map/ppermute | solution.py:14
  64.6 1.3 %collective-permute-start.3 = (f32[3,18,1,128]{3,2,1,0:T(1,128)S(1)}, f32[3,18,1,128]{3,2,1,0:T(1,128)S(1)}, u32[]{:S(2)}, u32[]{:S(2)}) collective-permute-start(f32[3,18,1,128]{3,2,1,0:T(1,128)S(1)} %get-tuple-element.35), channel_id=1, source_target_pairs={{1,0},{3,2},{5,4},{7,6},{9,8},{11,10},{13,12},{15,14},{17,16},{19,... | collective-permute-start | bytes 82952 | tf_op jit(solution)/shard_map/ppermute | solution.py:15
  65.9 0.2 fusion.12
  66.1 0.0 collective-permute-done.2
  66.1 4.2 %collective-permute-done.3 = f32[3,18,1,128]{3,2,1,0:T(1,128)S(1)} collective-permute-done((f32[3,18,1,128]{3,2,1,0:T(1,128)S(1)}, f32[3,18,1,128]{3,2,1,0:T(1,128)S(1)}, u32[]{:S(2)}, u32[]{:S(2)}) %collective-permute-start.3) | collective-permute-done | bytes 27680 | tf_op jit(solution)/shard_map/ppermute | solution.py:15
  70.4 0.1 pad_maximum_fusion
  70.5 0.2 fusion.8
  70.7 0.1 fusion.14
  70.8 0.8 %pad_maximum_fusion.1 = f32[3,16,16,128]{3,2,1,0:T(8,128)} fusion(f32[1,16,16,128]{3,2,1,0:T(8,128)S(1)} %fusion.14, f32[1,16,16,128]{3,2,1,0:T(8,128)S(1)} %fusion.12, f32[1,16,16,128]{3,2,1,0:T(8,128)S(1)} %fusion.8), kind=kLoop, calls=%fused_computation.12 | loop fusion | flops 196608 | bytes 786432 | tf_op jit(solution)/shard_map/stack | solution.py:36
  71.6 2.1 %copy.51 = f32[3,16,16,128]{2,1,0,3:T(8,128)S(1)} copy(f32[3,16,16,128]{3,2,1,0:T(8,128)} %pad_maximum_fusion.1) | data formatting | bytes 786432 | tf_op jit(solution)/shard_map/stack | solution.py:36
  73.7 1.8 %copy.54 = f32[3,16,16,128]{3,2,1,0:T(8,128)} copy(f32[3,16,16,128]{2,1,0,3:T(8,128)S(1)} %fusion.31) | data formatting | bytes 786432
  (15 shorter events, 0.2 us)
Async XLA Ops:
  0.6 32.6 %copy-start = (bf16[16,1,2,1536]{3,2,1,0:T(2,128)(2,1)S(1)}, bf16[16,1,2,1536]{3,2,1,0:T(2,128)(2,1)}, u32[]{:S(2)}) copy-start(bf16[16,1,2,1536]{3,2,1,0:T(2,128)(2,1)} %param.20) | copy-start | bytes 294916
  0.6 7.9 %copy-start.5 = (s32[1,1,1536]{2,1,0:T(1,128)S(1)}, s32[1,1,1536]{2,1,0:T(1,128)}, u32[]{:S(2)}) copy-start(s32[1,1,1536]{2,1,0:T(1,128)} %param.19) | copy-start | bytes 18436
  0.7 7.9 %copy-start.4 = (f32[1,1,1536]{2,1,0:T(1,128)S(1)}, f32[1,1,1536]{2,1,0:T(1,128)}, u32[]{:S(2)}) copy-start(f32[1,1,1536]{2,1,0:T(1,128)} %param.16) | copy-start | bytes 18436
  0.7 32.6 %copy-start.8 = (bf16[16,16,1,1536]{3,1,2,0:T(8,128)(2,1)S(1)}, bf16[16,16,1,1536]{3,1,2,0:T(8,128)(2,1)}, u32[]{:S(2)}) copy-start(bf16[16,16,1,1536]{3,1,2,0:T(8,128)(2,1)} %param.21) | copy-start | bytes 2359300
  2.1 58.4 %collective-permute-start = (f32[3,1,16,128]{3,2,1,0:T(8,128)}, f32[3,1,16,128]{3,2,1,0:T(8,128)}, u32[]{:S(2)}, u32[]{:S(2)}) collective-permute-start(f32[3,1,16,128]{3,2,1,0:T(8,128)} %get-tuple-element.42), channel_id=1, source_target_pairs={{0,2},{2,4},{4,6},{6,8},{8,10},{10,12},{12,14},{14,16},{16,18},{18... | collective-permute-start | bytes 73736 | tf_op jit(solution)/shard_map/ppermute | solution.py:14
  5.1 56.3 %collective-permute-start.1 = (f32[3,1,16,128]{3,2,1,0:T(8,128)}, f32[3,1,16,128]{3,2,1,0:T(8,128)}, u32[]{:S(2)}, u32[]{:S(2)}) collective-permute-start(f32[3,1,16,128]{3,2,1,0:T(8,128)} %get-tuple-element.41), channel_id=1, source_target_pairs={{2,0},{4,2},{6,4},{8,6},{10,8},{12,10},{14,12},{16,14},{18,16},{20... | collective-permute-start | bytes 73736 | tf_op jit(solution)/shard_map/ppermute | solution.py:15
  42.5 8.5 %copy-start.9 = (u32[32]{0:T(128)S(1)}, u32[32]{0:T(128)}, u32[]{:S(2)}) copy-start(u32[32]{0:T(128)} %constant.72) | copy-start | bytes 388
  42.5 9.1 %copy-start.6 = (f32[1,1,1536]{2,1,0:T(1,128)S(1)}, f32[1,1,1536]{2,1,0:T(1,128)}, u32[]{:S(2)}) copy-start(f32[1,1,1536]{2,1,0:T(1,128)} %param.18) | copy-start | bytes 18436
  42.5 9.1 %copy-start.7 = (f32[1,1,1536]{2,1,0:T(1,128)S(1)}, f32[1,1,1536]{2,1,0:T(1,128)}, u32[]{:S(2)}) copy-start(f32[1,1,1536]{2,1,0:T(1,128)} %param.17) | copy-start | bytes 18436
  42.5 17.2 %copy-start.1 = (f32[3,16,16,128]{3,2,1,0:T(8,128)S(1)}, f32[3,16,16,128]{3,2,1,0:T(8,128)}, u32[]{:S(2)}) copy-start(f32[3,16,16,128]{3,2,1,0:T(8,128)} %param.13) | copy-start | bytes 1179652
  42.5 23.4 %copy-start.3 = (f32[3,3,16,16,128]{4,3,2,1,0:T(8,128)S(1)}, f32[3,3,16,16,128]{4,3,2,1,0:T(8,128)}, u32[]{:S(2)}) copy-start(f32[3,3,16,16,128]{4,3,2,1,0:T(8,128)} %param.14) | copy-start | bytes 3538948
  50.9 15.0 %copy-start.2 = (f32[6,2,16,16,128]{4,3,2,1,0:T(8,128)S(1)}, f32[6,2,16,16,128]{4,3,2,1,0:T(8,128)}, u32[]{:S(2)}) copy-start(f32[6,2,16,16,128]{4,3,2,1,0:T(8,128)} %param.15) | copy-start | bytes 4718596
  62.2 4.0 %collective-permute-start.2 = (f32[3,18,1,128]{3,2,1,0:T(1,128)S(1)}, f32[3,18,1,128]{3,2,1,0:T(1,128)S(1)}, u32[]{:S(2)}, u32[]{:S(2)}) collective-permute-start(f32[3,18,1,128]{3,2,1,0:T(1,128)S(1)} %get-tuple-element.34), channel_id=1, source_target_pairs={{0,1},{2,3},{4,5},{6,7},{8,9},{10,11},{12,13},{14,15},{16,17},{18,... | collective-permute-start | bytes 82952 | tf_op jit(solution)/shard_map/ppermute | solution.py:14
  64.6 5.8 %collective-permute-start.3 = (f32[3,18,1,128]{3,2,1,0:T(1,128)S(1)}, f32[3,18,1,128]{3,2,1,0:T(1,128)S(1)}, u32[]{:S(2)}, u32[]{:S(2)}) collective-permute-start(f32[3,18,1,128]{3,2,1,0:T(1,128)S(1)} %get-tuple-element.35), channel_id=1, source_target_pairs={{1,0},{3,2},{5,4},{7,6},{9,8},{11,10},{13,12},{15,14},{17,16},{19,... | collective-permute-start | bytes 82952 | tf_op jit(solution)/shard_map/ppermute | solution.py:15
where the time goes:
time: 75.9 us; the launch traced here: 75.5 us
  blocking collectives  32.7 us (43%)
  local copies, waits for them, and re-layouts  25.7 us (34%)
  starting transfers between devices  7.98 us (11%)
  waiting for transfers between devices  4.27 us (6%)
  other arithmetic  2.72 us (4%)
  matrix products  1.12 us (1%)
  between operations  0.9 us (1%)
    all_gather x1, blocking collectives, on_device(): gathered = lax.all_gather(boundary_half, 'gx', axis=0, tiled=True)  24.6 us
    gather x1, local copies, waits for them, and re-layouts, on_device(): edge_trace = surface[owner_flat].reshape(boundary_field.shape)  8.39 us
    unnamed x1, blocking collectives  8.11 us
    scatter x1, local copies, waits for them, and re-layouts, on_device(): placed = jnp.zeros((boundary_count,), jnp.float32).at[owner_flat].set((co...  6.18 us
    ppermute x2, starting transfers between devices, with_halo(): before = lax.ppermute(last, axis, up)  5.41 us
    ppermute x2, waiting for transfers between devices, with_halo(): after = lax.ppermute(initial, axis, down)  4.23 us
    unnamed x26, local copies, waits for them, and re-layouts  4.02 us
    ppermute x2, starting transfers between devices, with_halo(): after = lax.ppermute(initial, axis, down)  2.57 us
  transfers between devices with their start and end apart: 4, of which 1 were waited for; matrix products, arithmetic and copies ran while one was open for 29% of the time, Pallas kernels for 0%

commit v1 on v0

v1 whole, which is shorter than its diff:
```python
import functools

import jax
import jax.numpy as jnp
from jax import lax
from jax.experimental import pallas as pl
from jax.experimental.pallas import tpu as pltpu
from jax.sharding import PartitionSpec as P

LANES = 128
NT = (((1,), (1,)), ((), ()))


def split3(value):
    top = value.astype(jnp.bfloat16)
    rest = value - top.astype(jnp.float32)
    mid = rest.astype(jnp.bfloat16)
    low = (rest - mid.astype(jnp.float32)).astype(jnp.bfloat16)
    return top, mid, low


def payload_kernel(x_index, y_index, field, boundary, core_out, outer_out, y_out):
    rows = boundary.shape[1] // LANES
    head = core_out.shape[0] - outer_out.shape[0]
    cells_x, cells_y = field.shape[1], field.shape[2]
    even_x = x_index[0] % 2 == 0
    even_y = y_index[0] % 2 == 0
    inner = jnp.where(even_x, cells_x - 1, 0)
    outer = cells_x - 1 - inner
    core_out[0:head, :] = jnp.zeros((head, LANES), jnp.float32)
    for q in range(rows):
        core_out[q : q + 1, :] = boundary[:, q * LANES : (q + 1) * LANES]
    for slot, comp in enumerate((1, 2)):
        at = slot * cells_y
        core_out[head + at : head + at + cells_y, :] = field[comp, inner]
        outer_out[at : at + cells_y, :] = field[comp, outer]
    for slot, comp in enumerate((0, 2)):
        for x in range(cells_x):
            high = field[comp, x, cells_y - 1 : cells_y, :]
            low = field[comp, x, 0:1, :]
            at = slot * cells_x + x
            y_out[0, at : at + 1, :] = jnp.where(even_y, high, low)
            if y_out.shape[0] == 2:
                y_out[1, at : at + 1, :] = jnp.where(even_y, low, high)


def volume_kernel(
    x_index,
    y_index,
    field,
    diag,
    face,
    x_inner,
    x_outer,
    y_halo,
    boundary,
    self_term,
    coupling,
    owner,
    volume_out,
    base_out,
):
    _, cells_x, cells_y, cells_z = field.shape
    count = boundary.shape[1]
    blocks = count // LANES
    half = blocks // 2
    per_block = LANES // cells_y
    padded = -(-blocks // 16) * 16
    head = x_inner.shape[0] - x_outer.shape[0]
    even_x = x_index[0] % 2 == 0
    even_y = y_index[0] % 2 == 0

    slot_of = owner[...]
    lane_of = slot_of % LANES
    block_of = slot_of // LANES
    onehot = (
        (lane_of == lax.broadcasted_iota(jnp.int32, (LANES, count), 0))
        .astype(jnp.float32)
        .astype(jnp.bfloat16)
    )
    in_block = block_of == lax.broadcasted_iota(jnp.int32, (padded, count), 0)

    spread = jnp.where(in_block, coupling[...] * boundary[...], 0.0)
    placed = jnp.zeros((LANES, padded), jnp.float32)
    for term in split3(spread):
        placed += lax.dot_general(onehot, term, NT, preferred_element_type=jnp.float32)

    ends = lax.broadcasted_iota(jnp.int32, (16, cells_z), 0)
    lane = lax.broadcasted_iota(jnp.int32, (16, cells_z), 1)
    pick = (
        (((ends == 0) & (lane == 0)) | ((ends == 1) & (lane == cells_z - 1)))
        .astype(jnp.float32)
        .astype(jnp.bfloat16)
    )
    flat = field[...].reshape(3 * cells_x * cells_y, cells_z)
    surface = jnp.zeros((16, 3 * cells_x * cells_y), jnp.float32)
    for term in split3(flat):
        surface += lax.dot_general(pick, term, NT, preferred_element_type=jnp.float32)
    table = jnp.concatenate(
        [
            surface[e : e + 1, b * LANES : (b + 1) * LANES]
            for e in range(2)
            for b in range(half)
        ]
        + [jnp.zeros((padded - blocks, LANES), jnp.float32)],
        axis=0,
    )
    read = jnp.zeros((padded, count), jnp.float32)
    for term in split3(table):
        read += jnp.dot(term, onehot, preferred_element_type=jnp.float32)
    trace = jnp.sum(jnp.where(in_block, read, 0.0), axis=0, keepdims=True)
    base_out[...] = self_term[...] * boundary[...] + coupling[...] * trace

    z_at = lax.broadcasted_iota(jnp.int32, (cells_y, cells_z), 1)
    y_at = lax.broadcasted_iota(jnp.int32, (cells_y, cells_z), 0)
    first_z, last_z = z_at == 0, z_at == cells_z - 1
    first_y, last_y = y_at == 0, y_at == cells_y - 1
    for x in range(cells_x):
        own = [field[c, x] for c in range(3)]
        x_plus, x_minus = {}, {}
        for slot, comp in enumerate((1, 2)):
            near = x_inner[head + slot * cells_y : head + (slot + 1) * cells_y, :]
            far = x_outer[slot * cells_y : (slot + 1) * cells_y, :]
            if x + 1 < cells_x:
                x_plus[comp] = field[comp, x + 1]
            else:
                x_plus[comp] = jnp.where(even_x, near, far)
            if x > 0:
                x_minus[comp] = field[comp, x - 1]
            else:
                x_minus[comp] = jnp.where(even_x, far, near)
        y_plus, y_minus = {}, {}
        for slot, comp in enumerate((0, 2)):
            at = slot * cells_x + x
            near = y_halo[0, at : at + 1, :]
            if y_halo.shape[0] == 2:
                far = y_halo[1, at : at + 1, :]
            else:
                far = jnp.zeros_like(near)
            above = jnp.where(even_y, near, far)
            below = jnp.where(even_y, far, near)
            y_plus[comp] = jnp.where(last_y, above, pltpu.roll(own[comp], cells_y - 1, 0))
            y_minus[comp] = jnp.where(first_y, below, pltpu.roll(own[comp], 1, 0))
        z_plus, z_minus = {}, {}
        for comp in (0, 1):
            z_plus[comp] = jnp.where(last_z, 0.0, pltpu.roll(own[comp], cells_z - 1, 1))
            z_minus[comp] = jnp.where(first_z, 0.0, pltpu.roll(own[comp], 1, 1))
        total = []
        for comp in range(3):
            total.append(
                diag[comp, 0, x] * own[0] + diag[comp, 1, x] * own[1] + diag[comp, 2, x] * own[2]
            )
        steps = (x_plus, x_minus, y_plus, y_minus, z_plus, z_minus)
        for offset, step in enumerate(steps):
            direction = offset // 2
            for slot, comp in enumerate(c for c in range(3) if c != direction):
                total[comp] = total[comp] - face[offset, slot, x] * step[comp]
        for comp in range(3):
            row = (comp * cells_x + x) * cells_y
            block, at = row // LANES, row % LANES
            bottom = placed[at : at + cells_y, block : block + 1]
            top = placed[at : at + cells_y, half + block : half + block + 1]
            total[comp] = total[comp] + jnp.where(
                first_z, bottom, jnp.where(last_z, top, 0.0)
            )
            volume_out[comp, x] = total[comp]


def integral_kernel(x_index, y_index, mine, theirs, right, left, base, own_out, send_out, stack, partial_value):
    columns = left.shape[1]
    rank, groups = right.shape[0], right.shape[1]
    count = right.shape[2]
    held = mine.shape[0]
    pitch = mine.shape[1]
    stack[0 : held * pitch, :] = mine[...].astype(jnp.float32).reshape(held * pitch, LANES)
    stack[held * pitch :, :] = theirs[...].astype(jnp.float32).reshape(held * pitch, LANES)
    pieces = [stack[pl.ds(q, groups, stride=pitch), :] for q in range(count // LANES)]
    gathered = jnp.concatenate(pieces, axis=1).astype(jnp.bfloat16)
    table = right[...].reshape(rank * groups, count)
    product = lax.dot_general(table, gathered, NT, preferred_element_type=jnp.float32)
    product = product.reshape(rank, groups, groups)
    source = lax.broadcasted_iota(jnp.int32, (rank, groups, groups), 2) ^ x_index[0]
    group = lax.broadcasted_iota(jnp.int32, (rank, groups, groups), 1)
    product = jnp.where(source == group, product, 0.0)
    coef = jnp.sum(jnp.sum(product, axis=1, keepdims=True), axis=2, keepdims=True)
    coef = coef.astype(jnp.bfloat16).astype(jnp.float32)
    total = jnp.zeros((columns, count), jnp.float32)
    for r in range(rank):
        total = total + coef[r] * left[r].astype(jnp.float32)
    partial_value[...] = total
    me = y_index[0]
    own_out[...] = base[...] + partial_value[pl.ds(me, 1), :]
    for step in range(1, columns):
        to = lax.rem(me + step, columns)
        send_out[step - 1] = partial_value[pl.ds(to, 1), :]


def on_device(
    n_x,
    n_y,
    volume_field,
    diag_blocks,
    face_weights,
    boundary_field,
    self_term,
    coupling,
    owner_map,
    left_basis,
    right_basis,
):
    f32 = jnp.float32
    _, cells_x, cells_y, cells_z = volume_field.shape
    count = boundary_field.shape[2]
    rank = left_basis.shape[0]
    rows = count // LANES
    head = -(-rows // 16) * 16
    x_index = lax.axis_index("gx").reshape(1)
    y_index = lax.axis_index("gy").reshape(1)
    boundary = boundary_field.reshape(1, count)
    vmem = pl.BlockSpec(memory_space=pltpu.VMEM)
    smem = pl.BlockSpec(memory_space=pltpu.SMEM)
    y_sides = 1 if n_y == 2 else 2

    def call(body, outs, n_in, scratch=()):
        return pl.pallas_call(
            body,
            out_shape=outs,
            in_specs=[smem, smem] + [vmem] * n_in,
            out_specs=[vmem] * len(outs),
            scratch_shapes=scratch,
            name=body.__name__,
        )

    def inner_pairs(size):
        return [(i, i ^ 1) for i in range(size)]

    def outer_pairs(size):
        up = [(i, i + 1) for i in range(1, size - 1, 2)]
        return up + [(j, i) for i, j in up]

    core_pay, outer_pay, y_pay = call(
        payload_kernel,
        [
            jax.ShapeDtypeStruct((head + 2 * cells_y, LANES), f32),
            jax.ShapeDtypeStruct((2 * cells_y, LANES), f32),
            jax.ShapeDtypeStruct((y_sides, 2 * cells_x, LANES), f32),
        ],
        2,
    )(x_index, y_index, volume_field, boundary)

    core_got = lax.ppermute(core_pay, "gx", inner_pairs(n_x))
    x_outer = lax.ppermute(outer_pay, "gx", outer_pairs(n_x))
    y_halo = lax.ppermute(y_pay[0], "gy", inner_pairs(n_y))[None]
    if y_sides == 2:
        y_far = lax.ppermute(y_pay[1], "gy", outer_pairs(n_y))[None]
        y_halo = jnp.concatenate([y_halo, y_far], axis=0)

    mine = core_pay[:head].astype(jnp.bfloat16)[None]
    theirs = core_got[:head].astype(jnp.bfloat16)[None]
    step = 2
    while step < n_x:
        mine = jnp.concatenate([mine, theirs], axis=0)
        theirs = lax.ppermute(mine, "gx", [(i, i ^ step) for i in range(n_x)])
        step *= 2

    volume_out, base = call(
        volume_kernel,
        [
            jax.ShapeDtypeStruct(volume_field.shape, f32),
            jax.ShapeDtypeStruct((1, count), f32),
        ],
        10,
    )(
        x_index,
        y_index,
        volume_field,
        diag_blocks,
        face_weights,
        core_got,
        x_outer,
        y_halo,
        boundary,
        self_term.reshape(1, count),
        coupling.reshape(1, count),
        owner_map.reshape(1, count),
    )

    own, send = call(
        integral_kernel,
        [
            jax.ShapeDtypeStruct((1, count), f32),
            jax.ShapeDtypeStruct((n_y - 1, 1, count), f32),
        ],
        5,
        [
            pltpu.VMEM((n_x * head, LANES), f32),
            pltpu.VMEM((n_y, count), f32),
        ],
    )(
        x_index,
        y_index,
        mine,
        theirs,
        right_basis.reshape(rank, n_x, count),
        left_basis.reshape(rank, n_y, count),
        base,
    )
    total = own
    for shift in range(1, n_y):
        pairs = [(i, (i + shift) % n_y) for i in range(n_y)]
        total = total + lax.ppermute(send[shift - 1], "gy", pairs)
    return volume_out, total.reshape(boundary_field.shape)


def solution(mesh):
    body = functools.partial(on_device, mesh.shape["gx"], mesh.shape["gy"])
    return jax.shard_map(
        body,
        mesh=mesh,
        in_specs=(
            P(None, "gx", "gy", None),
            P(None, None, "gx", "gy", None),
            P(None, None, "gx", "gy", None),
            P("gx", "gy", None),
            P("gx", "gy", None),
            P("gx", "gy", None),
            P("gx", "gy", None),
            P("gy", "gx", None, None),
            P("gx", None, "gy", None),
        ),
        out_specs=(P(None, "gx", "gy", None), P("gx", "gy", None)),
        check_vma=False,
    )
```

time: 75.9 us -> 32.8 us (0.43)
  blocking collectives: 32.7 us -> 0 us
  local copies, waits for them, and re-layouts: 25.7 us -> 1.91 us
  Pallas kernels: 0 us -> 7.76 us
  starting transfers between devices: 7.98 us -> 12.3 us
  waiting for transfers between devices: 4.27 us -> 8.46 us
  other arithmetic: 2.72 us -> 1.31 us
  matrix products: 1.12 us -> 0 us
    all_gather x1 -> x0, blocking collectives: 24.6 us -> none  [on_device(): gathered = lax.all_gather(boundary_half, 'gx', axis=0, tiled=True)]
    gather x1 -> x0, local copies, waits for them, and re-layouts: 8.39 us -> none  [on_device(): edge_trace = surface[owner_flat].reshape(boundary_field.shape)]
    unnamed x1 -> x0, blocking collectives: 8.11 us -> none
    pallas_call x0 -> x3, Pallas kernels: none -> 7.76 us  [the longest x1 3.82 us: on_device(): call(volume_kernel, [jax.ShapeDtypeStruct(volume_field.shape, f32), jax.S...]
    scatter x1 -> x0, local copies, waits for them, and re-layouts: 6.18 us -> none  [on_device(): placed = jnp.zeros((boundary_count,), jnp.float32).at[owner_flat].set((co...]
    ppermute x4 -> x7, starting transfers between devices: 7.98 us -> 12.3 us  [the longest x3 8.09 us: on_device(): theirs = lax.ppermute(mine, 'gx', [(i, i ^ step) for i in range(n_x)])]
    ppermute x4 -> x7, waiting for transfers between devices: 4.27 us -> 8.46 us  [the longest x3 3.35 us: on_device(): theirs = lax.ppermute(mine, 'gx', [(i, i ^ step) for i in range(n_x)])]
    slice x6 -> x0, local copies, waits for them, and re-layouts: 3.43 us -> none  [the longest x1 1.45 us: with_halo(): initial = lax.slice_in_dim(value, 0, width, axis=dim)]
  transfers between devices with their start and end apart: 4 -> 7, of which waited for: 1 -> 5; matrix products, arithmetic and copies ran while one was open for 29% -> 2% of each run, Pallas kernels for 0% -> 12%
where the time goes in v1:
time: 32.8 us; the launch traced here: 32.4 us
  starting transfers between devices  12.3 us (38%)
  waiting for transfers between devices  8.46 us (26%)
  Pallas kernels  7.76 us (24%)
  local copies, waits for them, and re-layouts  1.91 us (6%)
  other arithmetic  1.31 us (4%)
  between operations  0.67 us (2%)
    ppermute x3, starting transfers between devices, on_device(): theirs = lax.ppermute(mine, 'gx', [(i, i ^ step) for i in range(n_x)])  8.09 us
    pallas_call x1, Pallas kernels, on_device(): call(volume_kernel, [jax.ShapeDtypeStruct(volume_field.shape, f32), jax.S...  3.82 us
    ppermute x3, waiting for transfers between devices, on_device(): theirs = lax.ppermute(mine, 'gx', [(i, i ^ step) for i in range(n_x)])  3.35 us
    ppermute x1, waiting for transfers between devices, on_device(): y_halo = lax.ppermute(y_pay[0], 'gy', inner_pairs(n_y))[None]  2.42 us
    ppermute x1, waiting for transfers between devices, on_device(): total = total + lax.ppermute(send[shift - 1], 'gy', pairs)  2.32 us
    pallas_call x1, Pallas kernels, on_device(): call(integral_kernel, [jax.ShapeDtypeStruct((1, count), f32), jax.ShapeDt...  2.3 us
    pallas_call x1, Pallas kernels, on_device(): call(payload_kernel, [jax.ShapeDtypeStruct((head + 2 * cells_y, LANES), f...  1.64 us
    ppermute x1, starting transfers between devices, on_device(): y_halo = lax.ppermute(y_pay[0], 'gy', inner_pairs(n_y))[None]  1.58 us
  transfers between devices with their start and end apart: 7, of which 5 were waited for; matrix products, arithmetic and copies ran while one was open for 2% of the time, Pallas kernels for 12%

profile of v1, /device:TPU:0, one launch (start us, length us, event | category | flops | bytes accessed | tf_op | source)
XLA Modules:
  0.0 32.4 jit_solution(9967586570596740621)
XLA Ops:
  0.6 1.6 %payload_kernel.1 = (f32[48,128]{1,0:T(8,128)}, f32[32,128]{1,0:T(8,128)}, f32[1,32,128]{2,1,0:T(8,128)}) custom-call(s32[1]{0:T(128)} %bitcast.x_index, s32[1]{0:T(128)} %bitcast.1.y_index, f32[3,16,16,128]{3,2,1,0:T(8,128)} %field.3, f32[1,1536]{1,0:T(1,128)} %bitcast.19), custom_call_target="tpu_custom_call" | custom-call | tf_op jit(solution)/shard_map/payload_kernel/pallas_call | solution.py:241
  2.3 0.5 %collective-permute-start = (f32[48,128]{1,0:T(8,128)}, f32[48,128]{1,0:T(8,128)S(1)}, u32[]{:S(2)}, u32[]{:S(2)}) collective-permute-start(f32[48,128]{1,0:T(8,128)} %get-tuple-element.9), channel_id=1, source_target_pairs={{0,2},{2,0},{4,6},{6,4},{8,10},{10,8},{12,14},{14,12},{16,18},{18,... | collective-permute-start | bytes 73736 | tf_op jit(solution)/shard_map/ppermute | solution.py:251
  2.8 0.7 %fusion = bf16[1,16,128]{2,1,0:T(8,128)(2,1)S(1)} fusion(f32[48,128]{1,0:T(8,128)} %get-tuple-element.9), kind=kLoop, calls=%fused_computation.6 | loop fusion | bytes 8192 | tf_op jit(solution)/shard_map/broadcast_in_dim | solution.py:258
  3.5 0.4 %collective-permute-done.x_inner = f32[48,128]{1,0:T(8,128)S(1)} collective-permute-done((f32[48,128]{1,0:T(8,128)}, f32[48,128]{1,0:T(8,128)S(1)}, u32[]{:S(2)}, u32[]{:S(2)}) %collective-permute-start) | collective-permute-done | bytes 24608 | tf_op jit(solution)/shard_map/ppermute | solution.py:251
  3.8 0.0 copy-start.1
  3.8 2.9 %collective-permute-start.3 = (bf16[2,16,128]{2,1,0:T(8,128)(2,1)S(1)}, bf16[2,16,128]{2,1,0:T(8,128)(2,1)S(1)}, u32[]{:S(2)}, u32[]{:S(2)}) collective-permute-start(bf16[2,16,128]{2,1,0:T(8,128)(2,1)S(1)} %pad_maximum_fusion.2), channel_id=1, source_target_pairs={{0,4},{2,6},{4,0},{6,2},{8,12},{10,14},{12,8},{14,10},{16,20},{18,... | collective-permute-start | bytes 24584 | tf_op jit(solution)/shard_map/ppermute | solution.py:263
  6.7 1.6 %collective-permute-done.3 = bf16[2,16,128]{2,1,0:T(8,128)(2,1)S(1)} collective-permute-done((bf16[2,16,128]{2,1,0:T(8,128)(2,1)S(1)}, bf16[2,16,128]{2,1,0:T(8,128)(2,1)S(1)}, u32[]{:S(2)}, u32[]{:S(2)}) %collective-permute-start.3) | collective-permute-done | bytes 8224 | tf_op jit(solution)/shard_map/ppermute | solution.py:263
  8.4 2.1 %collective-permute-start.4 = (bf16[4,16,128]{2,1,0:T(8,128)(2,1)S(1)}, bf16[4,16,128]{2,1,0:T(8,128)(2,1)S(1)}, u32[]{:S(2)}, u32[]{:S(2)}) collective-permute-start(bf16[4,16,128]{2,1,0:T(8,128)(2,1)S(1)} %pad_maximum_fusion.1), channel_id=1, source_target_pairs={{0,8},{2,10},{4,12},{6,14},{8,0},{10,2},{12,4},{14,6},{16,24},{18,... | collective-permute-start | bytes 49160 | tf_op jit(solution)/shard_map/ppermute | solution.py:263
  10.5 1.7 %collective-permute-done.4 = bf16[4,16,128]{2,1,0:T(8,128)(2,1)S(1)} collective-permute-done((bf16[4,16,128]{2,1,0:T(8,128)(2,1)S(1)}, bf16[4,16,128]{2,1,0:T(8,128)(2,1)S(1)}, u32[]{:S(2)}, u32[]{:S(2)}) %collective-permute-start.4) | collective-permute-done | bytes 16416 | tf_op jit(solution)/shard_map/ppermute | solution.py:263
  12.2 0.0 copy-start
  12.2 3.1 %collective-permute-start.5 = (bf16[8,16,128]{2,1,0:T(8,128)(2,1)S(1)}, bf16[8,16,128]{2,1,0:T(8,128)(2,1)S(1)}, u32[]{:S(2)}, u32[]{:S(2)}) collective-permute-start(bf16[8,16,128]{2,1,0:T(8,128)(2,1)S(1)} %pad_maximum_fusion.mine), channel_id=1, source_target_pairs={{0,16},{2,18},{4,20},{6,22},{8,24},{10,26},{12,28},{14,30},{16,0},... | collective-permute-start | bytes 98312 | tf_op jit(solution)/shard_map/ppermute | solution.py:263
  15.3 0.7 %collective-permute-start.1 = (f32[32,128]{1,0:T(8,128)}, f32[32,128]{1,0:T(8,128)S(1)}, u32[]{:S(2)}, u32[]{:S(2)}) collective-permute-start(f32[32,128]{1,0:T(8,128)} %get-tuple-element.10), channel_id=1, source_target_pairs={{2,4},{6,8},{10,12},{14,16},{18,20},{22,24},{26,28},{4,2},{8,6},{1... | collective-permute-start | bytes 49160 | tf_op jit(solution)/shard_map/ppermute | solution.py:252
  16.0 1.6 %collective-permute-start.2 = (f32[32,128]{1,0:T(8,128)}, f32[32,128]{1,0:T(8,128)S(1)}, u32[]{:S(2)}, u32[]{:S(2)}) collective-permute-start(f32[32,128]{1,0:T(8,128)} %bitcast.25), channel_id=1, source_target_pairs={{0,1},{1,0},{2,3},{3,2},{4,5},{5,4},{6,7},{7,6},{8,9},{9,8},{10,11... | collective-permute-start | bytes 49160 | tf_op jit(solution)/shard_map/ppermute | solution.py:253
  17.5 0.0 collective-permute-done.1.x_outer
  17.5 0.0 copy-start.3
  17.5 2.4 %collective-permute-done.2 = f32[32,128]{1,0:T(8,128)S(1)} collective-permute-done((f32[32,128]{1,0:T(8,128)}, f32[32,128]{1,0:T(8,128)S(1)}, u32[]{:S(2)}, u32[]{:S(2)}) %collective-permute-start.2) | collective-permute-done | bytes 16416 | tf_op jit(solution)/shard_map/ppermute | solution.py:253
  20.0 0.0 copy-start.4
  20.0 0.0 copy-done.1
  20.0 0.0 copy-done.3
  20.0 0.6 %copy-done.4 = f32[32,128]{1,0:T(8,128)} copy-done((f32[32,128]{1,0:T(8,128)}, f32[32,128]{1,0:T(8,128)S(1)}, u32[]{:S(2)}) %copy-start.4) | copy-done | bytes 16408
  20.6 3.8 %volume_kernel.1 = (f32[3,16,16,128]{3,2,1,0:T(8,128)}, f32[1,1536]{1,0:T(1,128)}) custom-call(s32[1]{0:T(128)} %bitcast.x_index, s32[1]{0:T(128)} %bitcast.1.y_index, f32[3,16,16,128]{3,2,1,0:T(8,128)} %field.3, f32[3,3,16,16,128]{4,3,2,1,0:T(8,128)} %diag.1, f32[6,2,16,16,128]{4,3,2,1,0:T(8,128)} %face.1, f32[48,128]{1,0:T(8,128)} %copy-done.1, ...), custom_call_target="tpu_custom_call" | custom-call | tf_op jit(solution)/shard_map/volume_kernel/pallas_call | solution.py:266
  24.4 0.0 copy-done
  24.4 0.0 collective-permute-done.5.theirs
  24.4 0.0 copy-start.2
  24.4 0.6 %copy-done.2 = bf16[8,16,128]{2,1,0:T(8,128)(2,1)} copy-done((bf16[8,16,128]{2,1,0:T(8,128)(2,1)}, bf16[8,16,128]{2,1,0:T(8,128)(2,1)S(1)}, u32[]{:S(2)}) %copy-start.2) | copy-done | bytes 32792
  25.0 2.3 %integral_kernel.1 = (f32[1,1536]{1,0:T(1,128)}, f32[1,1,1536]{2,1,0:T(1,128)}) custom-call(s32[1]{0:T(128)} %bitcast.x_index, s32[1]{0:T(128)} %bitcast.1.y_index, bf16[8,16,128]{2,1,0:T(8,128)(2,1)} %copy-done, bf16[8,16,128]{2,1,0:T(8,128)(2,1)} %copy-done.2, bf16[16,16,1536]{2,1,0:T(8,128)(2,1)} %bitcast.17, bf16[16,2,1536]{2,1,0:T(2,128)(2,1)} %bitcast.18, ...), custom_call_target="tpu_custom_call" | custom-call | tf_op jit(solution)/shard_map/integral_kernel/pallas_call | solution.py:288
  27.3 1.5 %collective-permute-start.6 = (f32[1,1536]{1,0:T(1,128)}, f32[1,1536]{1,0:T(1,128)S(1)}, u32[]{:S(2)}, u32[]{:S(2)}) collective-permute-start(f32[1,1536]{1,0:T(1,128)} %bitcast.26), channel_id=1, source_target_pairs={{0,1},{1,0},{2,3},{3,2},{4,5},{5,4},{6,7},{7,6},{8,9},{9,8},{10,11... | collective-permute-start | bytes 18440 | tf_op jit(solution)/shard_map/ppermute | solution.py:311
  28.8 2.3 %collective-permute-done.6 = f32[1,1536]{1,0:T(1,128)S(1)} collective-permute-done((f32[1,1536]{1,0:T(1,128)}, f32[1,1536]{1,0:T(1,128)S(1)}, u32[]{:S(2)}, u32[]{:S(2)}) %collective-permute-start.6) | collective-permute-done | bytes 6176 | tf_op jit(solution)/shard_map/ppermute | solution.py:311
  31.1 1.3 %add_bitcast_fusion = f32[1,1,1536]{2,1,0:T(1,128)} fusion(f32[1,1536]{1,0:T(1,128)} %get-tuple-element.14, f32[1,1536]{1,0:T(1,128)S(1)} %collective-permute-done.6), kind=kLoop, calls=%fused_computation.5 | loop fusion | flops 1536 | bytes 18432 | tf_op jit(solution)/shard_map/reshape | solution.py:312
  (4 shorter events, 0.0 us)
Async XLA Ops:
  2.3 1.6 %collective-permute-start = (f32[48,128]{1,0:T(8,128)}, f32[48,128]{1,0:T(8,128)S(1)}, u32[]{:S(2)}, u32[]{:S(2)}) collective-permute-start(f32[48,128]{1,0:T(8,128)} %get-tuple-element.9), channel_id=1, source_target_pairs={{0,2},{2,0},{4,6},{6,4},{8,10},{10,8},{12,14},{14,12},{16,18},{18,... | collective-permute-start | bytes 73736 | tf_op jit(solution)/shard_map/ppermute | solution.py:251
  3.8 16.1 %copy-start.1 = (f32[48,128]{1,0:T(8,128)}, f32[48,128]{1,0:T(8,128)S(1)}, u32[]{:S(2)}) copy-start(f32[48,128]{1,0:T(8,128)S(1)} %collective-permute-done.x_inner) | copy-start | bytes 73732
  3.8 4.5 %collective-permute-start.3 = (bf16[2,16,128]{2,1,0:T(8,128)(2,1)S(1)}, bf16[2,16,128]{2,1,0:T(8,128)(2,1)S(1)}, u32[]{:S(2)}, u32[]{:S(2)}) collective-permute-start(bf16[2,16,128]{2,1,0:T(8,128)(2,1)S(1)} %pad_maximum_fusion.2), channel_id=1, source_target_pairs={{0,4},{2,6},{4,0},{6,2},{8,12},{10,14},{12,8},{14,10},{16,20},{18,... | collective-permute-start | bytes 24584 | tf_op jit(solution)/shard_map/ppermute | solution.py:263
  8.4 3.8 %collective-permute-start.4 = (bf16[4,16,128]{2,1,0:T(8,128)(2,1)S(1)}, bf16[4,16,128]{2,1,0:T(8,128)(2,1)S(1)}, u32[]{:S(2)}, u32[]{:S(2)}) collective-permute-start(bf16[4,16,128]{2,1,0:T(8,128)(2,1)S(1)} %pad_maximum_fusion.1), channel_id=1, source_target_pairs={{0,8},{2,10},{4,12},{6,14},{8,0},{10,2},{12,4},{14,6},{16,24},{18,... | collective-permute-start | bytes 49160 | tf_op jit(solution)/shard_map/ppermute | solution.py:263
  12.2 12.2 %copy-start = (bf16[8,16,128]{2,1,0:T(8,128)(2,1)}, bf16[8,16,128]{2,1,0:T(8,128)(2,1)S(1)}, u32[]{:S(2)}) copy-start(bf16[8,16,128]{2,1,0:T(8,128)(2,1)S(1)} %pad_maximum_fusion.mine) | copy-start | bytes 98308
  12.2 12.2 %collective-permute-start.5 = (bf16[8,16,128]{2,1,0:T(8,128)(2,1)S(1)}, bf16[8,16,128]{2,1,0:T(8,128)(2,1)S(1)}, u32[]{:S(2)}, u32[]{:S(2)}) collective-permute-start(bf16[8,16,128]{2,1,0:T(8,128)(2,1)S(1)} %pad_maximum_fusion.mine), channel_id=1, source_target_pairs={{0,16},{2,18},{4,20},{6,22},{8,24},{10,26},{12,28},{14,30},{16,0},... | collective-permute-start | bytes 98312 | tf_op jit(solution)/shard_map/ppermute | solution.py:263
  15.3 2.2 %collective-permute-start.1 = (f32[32,128]{1,0:T(8,128)}, f32[32,128]{1,0:T(8,128)S(1)}, u32[]{:S(2)}, u32[]{:S(2)}) collective-permute-start(f32[32,128]{1,0:T(8,128)} %get-tuple-element.10), channel_id=1, source_target_pairs={{2,4},{6,8},{10,12},{14,16},{18,20},{22,24},{26,28},{4,2},{8,6},{1... | collective-permute-start | bytes 49160 | tf_op jit(solution)/shard_map/ppermute | solution.py:252
  16.0 4.0 %collective-permute-start.2 = (f32[32,128]{1,0:T(8,128)}, f32[32,128]{1,0:T(8,128)S(1)}, u32[]{:S(2)}, u32[]{:S(2)}) collective-permute-start(f32[32,128]{1,0:T(8,128)} %bitcast.25), channel_id=1, source_target_pairs={{0,1},{1,0},{2,3},{3,2},{4,5},{5,4},{6,7},{7,6},{8,9},{9,8},{10,11... | collective-permute-start | bytes 49160 | tf_op jit(solution)/shard_map/ppermute | solution.py:253
  17.5 2.4 %copy-start.3 = (f32[32,128]{1,0:T(8,128)}, f32[32,128]{1,0:T(8,128)S(1)}, u32[]{:S(2)}) copy-start(f32[32,128]{1,0:T(8,128)S(1)} %collective-permute-done.1.x_outer) | copy-start | bytes 49156
  20.0 0.6 %copy-start.4 = (f32[32,128]{1,0:T(8,128)}, f32[32,128]{1,0:T(8,128)S(1)}, u32[]{:S(2)}) copy-start(f32[32,128]{1,0:T(8,128)S(1)} %collective-permute-done.2) | copy-start | bytes 49156
  24.4 0.6 %copy-start.2 = (bf16[8,16,128]{2,1,0:T(8,128)(2,1)}, bf16[8,16,128]{2,1,0:T(8,128)(2,1)S(1)}, u32[]{:S(2)}) copy-start(bf16[8,16,128]{2,1,0:T(8,128)(2,1)S(1)} %collective-permute-done.5.theirs) | copy-start | bytes 98308
  27.3 3.8 %collective-permute-start.6 = (f32[1,1536]{1,0:T(1,128)}, f32[1,1536]{1,0:T(1,128)S(1)}, u32[]{:S(2)}, u32[]{:S(2)}) collective-permute-start(f32[1,1536]{1,0:T(1,128)} %bitcast.26), channel_id=1, source_target_pairs={{0,1},{1,0},{2,3},{3,2},{4,5},{5,4},{6,7},{7,6},{8,9},{9,8},{10,11... | collective-permute-start | bytes 18440 | tf_op jit(solution)/shard_map/ppermute | solution.py:311

commit v2 on v1

--- a/solution.py
+++ b/solution.py
@@ -19,56 +19,86 @@
     return top, mid, low
 
 
-def payload_kernel(x_index, y_index, field, boundary, core_out, outer_out, y_out):
-    rows = boundary.shape[1] // LANES
-    head = core_out.shape[0] - outer_out.shape[0]
+def halo_kernel(
+    x_index, y_index, field, boundary, inner_out, outer_out, y_out, boundary_out, sems
+):
     cells_x, cells_y = field.shape[1], field.shape[2]
-    even_x = x_index[0] % 2 == 0
-    even_y = y_index[0] % 2 == 0
-    inner = jnp.where(even_x, cells_x - 1, 0)
-    outer = cells_x - 1 - inner
-    core_out[0:head, :] = jnp.zeros((head, LANES), jnp.float32)
-    for q in range(rows):
-        core_out[q : q + 1, :] = boundary[:, q * LANES : (q + 1) * LANES]
+    inner = jnp.where(x_index[0] % 2 == 0, cells_x - 1, 0)
+    beside = jnp.where(y_index[0] % 2 == 0, cells_y - 1, 0)
+    copies = []
+
+    def copy(source, target):
+        copies.append(pltpu.make_async_copy(source, target, sems.at[len(copies)]))
+        copies[-1].start()
+
     for slot, comp in enumerate((1, 2)):
-        at = slot * cells_y
-        core_out[head + at : head + at + cells_y, :] = field[comp, inner]
-        outer_out[at : at + cells_y, :] = field[comp, outer]
-    for slot, comp in enumerate((0, 2)):
-        for x in range(cells_x):
-            high = field[comp, x, cells_y - 1 : cells_y, :]
-            low = field[comp, x, 0:1, :]
-            at = slot * cells_x + x
-            y_out[0, at : at + 1, :] = jnp.where(even_y, high, low)
-            if y_out.shape[0] == 2:
-                y_out[1, at : at + 1, :] = jnp.where(even_y, low, high)
+        rows = pl.ds(slot * cells_y, cells_y)
+        copy(field.at[comp, inner], inner_out.at[rows])
+        copy(field.at[comp, cells_x - 1 - inner], outer_out.at[rows])
+    for side in range(y_out.shape[0]):
+        row = beside if side == 0 else cells_y - 1 - beside
+        for slot, comp in enumerate((0, 2)):
+            rows = pl.ds(slot * cells_x, cells_x)
+            copy(field.at[comp, :, row], y_out.at[side, rows])
+    copy(boundary, boundary_out)
+    for one in copies:
+        one.wait()
+
+
+def pack_kernel(mine, theirs, out):
+    rows = mine.shape[1] // LANES
+    for i, source in enumerate((mine, theirs)):
+        lines = [source[:, q * LANES : (q + 1) * LANES] for q in range(rows)]
+        lines.append(jnp.zeros((out.shape[1] - rows, LANES), jnp.float32))
+        out[i] = jnp.concatenate(lines, axis=0).astype(jnp.bfloat16)
 
 
 def volume_kernel(
     x_index,
     y_index,
+    field_in,
+    diag_in,
+    face_in,
+    boundary_in,
+    self_in,
+    coupling_in,
+    owner_in,
+    x_inner,
+    x_outer,
+    y_halo,
+    volume_out,
+    base_out,
     field,
     diag,
     face,
-    x_inner,
-    x_outer,
-    y_halo,
     boundary,
     self_term,
     coupling,
     owner,
-    volume_out,
-    base_out,
+    sems,
 ):
+    pairs = (
+        (owner_in, owner),
+        (coupling_in, coupling),
+        (boundary_in, boundary),
+        (self_in, self_term),
+        (field_in, field),
+        (diag_in, diag),
+        (face_in, face),
+    )
+    loads = [pltpu.make_async_copy(a, b, sems.at[i]) for i, (a, b) in enumerate(pairs)]
+    for load in loads:
+        load.start()
     _, cells_x, cells_y, cells_z = field.shape
     count = boundary.shape[1]
     blocks = count // LANES
     half = blocks // 2
-    per_block = LANES // cells_y
     padded = -(-blocks // 16) * 16
-    head = x_inner.shape[0] - x_outer.shape[0]
     even_x = x_index[0] % 2 == 0
     even_y = y_index[0] % 2 == 0
+
+    for load in loads[:4]:
+        load.wait()
 
     slot_of = owner[...]
     lane_of = slot_of % LANES
@@ -92,6 +122,7 @@
         .astype(jnp.float32)
         .astype(jnp.bfloat16)
     )
+    loads[4].wait()
     flat = field[...].reshape(3 * cells_x * cells_y, cells_z)
     surface = jnp.zeros((16, 3 * cells_x * cells_y), jnp.float32)
     for term in split3(flat):
@@ -111,6 +142,8 @@
     trace = jnp.sum(jnp.where(in_block, read, 0.0), axis=0, keepdims=True)
     base_out[...] = self_term[...] * boundary[...] + coupling[...] * trace
 
+    for load in loads[5:]:
+        load.wait()
     z_at = lax.broadcasted_iota(jnp.int32, (cells_y, cells_z), 1)
     y_at = lax.broadcasted_iota(jnp.int32, (cells_y, cells_z), 0)
     first_z, last_z = z_at == 0, z_at == cells_z - 1
@@ -119,7 +152,7 @@
         own = [field[c, x] for c in range(3)]
         x_plus, x_minus = {}, {}
         for slot, comp in enumerate((1, 2)):
-            near = x_inner[head + slot * cells_y : head + (slot + 1) * cells_y, :]
+            near = x_inner[slot * cells_y : (slot + 1) * cells_y, :]
             far = x_outer[slot * cells_y : (slot + 1) * cells_y, :]
             if x + 1 < cells_x:
                 x_plus[comp] = field[comp, x + 1]
@@ -209,7 +242,7 @@
     right_basis,
 ):
     f32 = jnp.float32
-    _, cells_x, cells_y, cells_z = volume_field.shape
+    _, cells_x, cells_y, _ = volume_field.shape
     count = boundary_field.shape[2]
     rank = left_basis.shape[0]
     rows = count // LANES
@@ -219,17 +252,23 @@
     boundary = boundary_field.reshape(1, count)
     vmem = pl.BlockSpec(memory_space=pltpu.VMEM)
     smem = pl.BlockSpec(memory_space=pltpu.SMEM)
+    hbm = pl.BlockSpec(memory_space=pltpu.HBM)
     y_sides = 1 if n_y == 2 else 2
 
-    def call(body, outs, n_in, scratch=()):
+    def call(body, outs, args, scratch=(), far=0, indices=True):
+        lead = (x_index, y_index) if indices else ()
+        args = [
+            pltpu.with_memory_space_constraint(arg, pltpu.HBM if i < far else pltpu.VMEM)
+            for i, arg in enumerate(args)
+        ]
         return pl.pallas_call(
             body,
             out_shape=outs,
-            in_specs=[smem, smem] + [vmem] * n_in,
+            in_specs=[smem] * len(lead) + [hbm] * far + [vmem] * (len(args) - far),
             out_specs=[vmem] * len(outs),
             scratch_shapes=scratch,
-            name=body.__name__,
-        )
+            compiler_params=pltpu.CompilerParams(vmem_limit_bytes=16 * 2**20),
+        )(*lead, *args)
 
     def inner_pairs(size):
         return [(i, i ^ 1) for i in range(size)]
@@ -238,77 +277,90 @@
         up = [(i, i + 1) for i in range(1, size - 1, 2)]
         return up + [(j, i) for i, j in up]
 
-    core_pay, outer_pay, y_pay = call(
-        payload_kernel,
-        [
-            jax.ShapeDtypeStruct((head + 2 * cells_y, LANES), f32),
-            jax.ShapeDtypeStruct((2 * cells_y, LANES), f32),
-            jax.ShapeDtypeStruct((y_sides, 2 * cells_x, LANES), f32),
-        ],
-        2,
-    )(x_index, y_index, volume_field, boundary)
-
-    core_got = lax.ppermute(core_pay, "gx", inner_pairs(n_x))
+    core_got = lax.ppermute(boundary, "gx", inner_pairs(n_x))
+    inner_pay, outer_pay, y_pay, near_boundary = call(
+        halo_kernel,
+        [
+            pltpu.VMEM((2 * cells_y, LANES), f32),
+            pltpu.VMEM((2 * cells_y, LANES), f32),
+            pltpu.VMEM((y_sides, 2 * cells_x, LANES), f32),
+            pltpu.VMEM((1, count), f32),
+        ],
+        [volume_field, boundary],
+        [pltpu.SemaphoreType.DMA((5 + 2 * y_sides,))],
+        far=2,
+    )
+    x_inner = lax.ppermute(inner_pay, "gx", inner_pairs(n_x))
     x_outer = lax.ppermute(outer_pay, "gx", outer_pairs(n_x))
     y_halo = lax.ppermute(y_pay[0], "gy", inner_pairs(n_y))[None]
     if y_sides == 2:
         y_far = lax.ppermute(y_pay[1], "gy", outer_pairs(n_y))[None]
         y_halo = jnp.concatenate([y_halo, y_far], axis=0)
 
-    mine = core_pay[:head].astype(jnp.bfloat16)[None]
-    theirs = core_got[:head].astype(jnp.bfloat16)[None]
-    step = 2
+    (mine,) = call(
+        pack_kernel,
+        [pltpu.VMEM((2, head, LANES), jnp.bfloat16)],
+        [near_boundary, core_got],
+        indices=False,
+    )
+    theirs = lax.ppermute(mine, "gx", [(i, i ^ 2) for i in range(n_x)])
+    step = 4
     while step < n_x:
         mine = jnp.concatenate([mine, theirs], axis=0)
         theirs = lax.ppermute(mine, "gx", [(i, i ^ step) for i in range(n_x)])
         step *= 2
 
+    row = (1, count)
     volume_out, base = call(
         volume_kernel,
-        [
-            jax.ShapeDtypeStruct(volume_field.shape, f32),
-            jax.ShapeDtypeStruct((1, count), f32),
-        ],
-        10,
-    )(
-        x_index,
-        y_index,
-        volume_field,
-        diag_blocks,
-        face_weights,
-        core_got,
-        x_outer,
-        y_halo,
-        boundary,
-        self_term.reshape(1, count),
-        coupling.reshape(1, count),
-        owner_map.reshape(1, count),
-    )
-
-    own, send = call(
+        [pltpu.VMEM(volume_field.shape, f32), pltpu.VMEM(row, f32)],
+        [
+            volume_field,
+            diag_blocks,
+            face_weights,
+            boundary,
+            self_term.reshape(row),
+            coupling.reshape(row),
+            owner_map.reshape(row),
+            x_inner,
+            x_outer,
+            y_halo,
+        ],
+        [
+            pltpu.VMEM(volume_field.shape, f32),
+            pltpu.VMEM(diag_blocks.shape, f32),
+            pltpu.VMEM(face_weights.shape, f32),
+            pltpu.VMEM(row, f32),
+            pltpu.VMEM(row, f32),
+            pltpu.VMEM(row, f32),
+            pltpu.VMEM(row, jnp.int32),
+            pltpu.SemaphoreType.DMA((7,)),
+        ],
+        far=7,
+    )
+
+    own, shares = call(
         integral_kernel,
         [
-            jax.ShapeDtypeStruct((1, count), f32),
-            jax.ShapeDtypeStruct((n_y - 1, 1, count), f32),
-        ],
-        5,
+            pltpu.VMEM((1, count), f32),
+            pltpu.VMEM((n_y - 1, 1, count), f32),
+        ],
+        [
+            mine,
+            theirs,
+            right_basis.reshape(rank, n_x, count),
+            left_basis.reshape(rank, n_y, count),
+            base,
+        ],
         [
             pltpu.VMEM((n_x * head, LANES), f32),
             pltpu.VMEM((n_y, count), f32),
         ],
-    )(
-        x_index,
-        y_index,
-        mine,
-        theirs,
-        right_basis.reshape(rank, n_x, count),
-        left_basis.reshape(rank, n_y, count),
-        base,
     )
     total = own
     for shift in range(1, n_y):
         pairs = [(i, (i + shift) % n_y) for i in range(n_y)]
-        total = total + lax.ppermute(send[shift - 1], "gy", pairs)
+        total = total + lax.ppermute(shares[shift - 1], "gy", pairs)
     return volume_out, total.reshape(boundary_field.shape)
 
 

time: 32.8 us -> 27.7 us (0.84)
  the two profiles are of different devices: /device:TPU:0 before, /device:TPU:8 now
where the time goes in v2:
time: 27.7 us; the launch traced here: 27.4 us
  waiting for transfers between devices  11.3 us (41%)
  starting transfers between devices  9.7 us (35%)
  Pallas kernels  4.33 us (16%)
  local copies, waits for them, and re-layouts  0.75 us (3%)
  between operations  0.72 us (3%)
  other arithmetic  0.61 us (2%)
    pallas_call x4, Pallas kernels, call(): pl.pallas_call(body, out_shape=outs, in_specs=[smem] * len(lead) + [hbm]...  4.33 us
    ppermute x2, waiting for transfers between devices, on_device(): theirs = lax.ppermute(mine, 'gx', [(i, i ^ step) for i in range(n_x)])  3.74 us
    ppermute x1, starting transfers between devices, on_device(): x_outer = lax.ppermute(outer_pay, 'gx', outer_pairs(n_x))  3.39 us
    ppermute x2, starting transfers between devices, on_device(): theirs = lax.ppermute(mine, 'gx', [(i, i ^ step) for i in range(n_x)])  2.59 us
    ppermute x1, waiting for transfers between devices, on_device(): x_outer = lax.ppermute(outer_pay, 'gx', outer_pairs(n_x))  2.53 us
    ppermute x1, waiting for transfers between devices, on_device(): total = total + lax.ppermute(shares[shift - 1], 'gy', pairs)  2.38 us
    ppermute x1, waiting for transfers between devices, on_device(): theirs = lax.ppermute(mine, 'gx', [(i, i ^ 2) for i in range(n_x)])  2.16 us
    ppermute x1, starting transfers between devices, on_device(): theirs = lax.ppermute(mine, 'gx', [(i, i ^ 2) for i in range(n_x)])  1.56 us
  transfers between devices with their start and end apart: 8, of which 5 were waited for; matrix products, arithmetic and copies ran while one was open for 3% of the time, Pallas kernels for 14%

profile of v2, /device:TPU:8, one launch (start us, length us, event | category | flops | bytes accessed | tf_op | source)
XLA Modules:
  0.0 27.4 jit_solution(8125665917043569437)
XLA Ops:
  0.6 0.1 collective-permute-start.3
  0.7 0.9 %shard_map.104 = (f32[32,128]{1,0:T(8,128)S(1)}, f32[32,128]{1,0:T(8,128)S(1)}, f32[1,32,128]{2,1,0:T(8,128)S(1)}, f32[1,1536]{1,0:T(1,128)S(1)}) custom-call(s32[1]{0:T(128)} %bitcast.x_index, s32[1]{0:T(128)} %bitcast.1.y_index, f32[3,16,16,128]{3,2,1,0:T(8,128)} %field_in.1, f32[1,1536]{1,0:T(1,128)} %bitcast.19), custom_call_target="tpu_custom_call" | custom-call | tf_op jit(solution)/shard_map/pallas_call | solution.py:264
  1.6 0.5 %collective-permute-done.3.theirs = f32[1,1536]{1,0:T(1,128)S(1)} collective-permute-done((f32[1,1536]{1,0:T(1,128)}, f32[1,1536]{1,0:T(1,128)S(1)}, u32[]{:S(2)}, u32[]{:S(2)}) %collective-permute-start.3) | collective-permute-done | bytes 6176 | tf_op jit(solution)/shard_map/ppermute | solution.py:280
  2.1 1.6 %collective-permute-start.4 = (bf16[2,16,128]{2,1,0:T(8,128)(2,1)S(1)}, bf16[2,16,128]{2,1,0:T(8,128)(2,1)S(1)}, u32[]{:S(2)}, u32[]{:S(2)}) collective-permute-start(bf16[2,16,128]{2,1,0:T(8,128)(2,1)S(1)} %shard_map.106), channel_id=1, source_target_pairs={{0,4},{2,6},{4,0},{6,2},{8,12},{10,14},{12,8},{14,10},{16,20},{18,... | collective-permute-start | bytes 24584 | tf_op jit(solution)/shard_map/ppermute | solution.py:306
  3.6 2.2 %collective-permute-done.4 = bf16[2,16,128]{2,1,0:T(8,128)(2,1)S(1)} collective-permute-done((bf16[2,16,128]{2,1,0:T(8,128)(2,1)S(1)}, bf16[2,16,128]{2,1,0:T(8,128)(2,1)S(1)}, u32[]{:S(2)}, u32[]{:S(2)}) %collective-permute-start.4) | collective-permute-done | bytes 8224 | tf_op jit(solution)/shard_map/ppermute | solution.py:306
  5.8 0.0 collective-permute-start.5
  5.8 3.7 %collective-permute-done.5 = bf16[4,16,128]{2,1,0:T(8,128)(2,1)S(1)} collective-permute-done((bf16[4,16,128]{2,1,0:T(8,128)(2,1)S(1)}, bf16[4,16,128]{2,1,0:T(8,128)(2,1)S(1)}, u32[]{:S(2)}, u32[]{:S(2)}) %collective-permute-start.5) | collective-permute-done | bytes 16416 | tf_op jit(solution)/shard_map/ppermute | solution.py:310
  9.6 2.6 %collective-permute-start.6 = (bf16[8,16,128]{2,1,0:T(8,128)(2,1)S(1)}, bf16[8,16,128]{2,1,0:T(8,128)(2,1)S(1)}, u32[]{:S(2)}, u32[]{:S(2)}) collective-permute-start(bf16[8,16,128]{2,1,0:T(8,128)(2,1)S(1)} %pad_maximum_fusion.mine), channel_id=1, source_target_pairs={{0,16},{2,18},{4,20},{6,22},{8,24},{10,26},{12,28},{14,30},{16,0},... | collective-permute-start | bytes 98312 | tf_op jit(solution)/shard_map/ppermute | solution.py:310
  12.1 1.5 %collective-permute-start.2 = (f32[32,128]{1,0:T(8,128)S(1)}, f32[32,128]{1,0:T(8,128)S(1)}, u32[]{:S(2)}, u32[]{:S(2)}) collective-permute-start(f32[32,128]{1,0:T(8,128)S(1)} %bitcast.16), channel_id=1, source_target_pairs={{0,1},{1,0},{2,3},{3,2},{4,5},{5,4},{6,7},{7,6},{8,9},{9,8},{10,11... | collective-permute-start | bytes 49160 | tf_op jit(solution)/shard_map/ppermute | solution.py:295
  13.7 0.0 collective-permute-start
  13.7 3.4 %collective-permute-start.1 = (f32[32,128]{1,0:T(8,128)S(1)}, f32[32,128]{1,0:T(8,128)S(1)}, u32[]{:S(2)}, u32[]{:S(2)}) collective-permute-start(f32[32,128]{1,0:T(8,128)S(1)} %get-tuple-element.11), channel_id=1, source_target_pairs={{2,4},{6,8},{10,12},{14,16},{18,20},{22,24},{26,28},{4,2},{8,6},{1... | collective-permute-start | bytes 49160 | tf_op jit(solution)/shard_map/ppermute | solution.py:294
  17.1 0.0 collective-permute-done.2
  17.1 0.0 collective-permute-done.x_inner
  17.1 2.5 %collective-permute-done.1.x_outer = f32[32,128]{1,0:T(8,128)S(1)} collective-permute-done((f32[32,128]{1,0:T(8,128)S(1)}, f32[32,128]{1,0:T(8,128)S(1)}, u32[]{:S(2)}, u32[]{:S(2)}) %collective-permute-start.1) | collective-permute-done | bytes 16416 | tf_op jit(solution)/shard_map/ppermute | solution.py:294
  19.6 0.0 copy-start
  19.6 0.0 copy-start.1
  19.6 3.0 %shard_map.105 = (f32[3,16,16,128]{3,2,1,0:T(8,128)S(1)}, f32[1,1536]{1,0:T(1,128)S(1)}) custom-call(s32[1]{0:T(128)} %bitcast.x_index, s32[1]{0:T(128)} %bitcast.1.y_index, f32[3,16,16,128]{3,2,1,0:T(8,128)} %field_in.1, f32[3,3,16,16,128]{4,3,2,1,0:T(8,128)} %diag_in.1, f32[6,2,16,16,128]{4,3,2,1,0:T(8,128)} %face_in.1, f32[1,1536]{1,0:T(1,128)} %bitcast.20, ...), custom_call_target="tpu_custom_call" | custom-call | tf_op jit(solution)/shard_map/pallas_call | solution.py:264
  22.6 0.0 collective-permute-done.6.theirs
  22.6 0.0 copy-done
  22.7 0.0 copy-done.1
  22.7 0.5 %shard_map.107 = (f32[1,1536]{1,0:T(1,128)S(1)}, f32[1,1,1536]{2,1,0:T(1,128)S(1)}) custom-call(s32[1]{0:T(128)} %bitcast.x_index, s32[1]{0:T(128)} %bitcast.1.y_index, bf16[8,16,128]{2,1,0:T(8,128)(2,1)S(1)} %pad_maximum_fusion.mine, bf16[8,16,128]{2,1,0:T(8,128)(2,1)S(1)} %collective-permute-done.6.theirs, bf16[16,16,1536]{2,1,0:T(8,128)(2,1)S(1)} %bitcast.13, ...), custom_call_target="tpu_custom_call" | custom-call | tf_op jit(solution)/shard_map/pallas_call | solution.py:264
  23.1 0.6 %collective-permute-start.7 = (f32[1,1536]{1,0:T(1,128)S(1)}, f32[1,1536]{1,0:T(1,128)S(1)}, u32[]{:S(2)}, u32[]{:S(2)}) collective-permute-start(f32[1,1536]{1,0:T(1,128)S(1)} %bitcast.17), channel_id=1, source_target_pairs={{0,1},{1,0},{2,3},{3,2},{4,5},{5,4},{6,7},{7,6},{8,9},{9,8},{10,11... | collective-permute-start | bytes 18440 | tf_op jit(solution)/shard_map/ppermute | solution.py:363
  23.7 0.7 %copy.11 = f32[3,16,16,128]{3,2,1,0:T(8,128)} copy(f32[3,16,16,128]{3,2,1,0:T(8,128)S(1)} %get-tuple-element.18) | data formatting | bytes 786432
  24.4 2.4 %collective-permute-done.7 = f32[1,1536]{1,0:T(1,128)S(1)} collective-permute-done((f32[1,1536]{1,0:T(1,128)S(1)}, f32[1,1536]{1,0:T(1,128)S(1)}, u32[]{:S(2)}, u32[]{:S(2)}) %collective-permute-start.7) | collective-permute-done | bytes 6176 | tf_op jit(solution)/shard_map/ppermute | solution.py:363
  26.8 0.6 %add_bitcast_fusion = f32[1,1,1536]{2,1,0:T(1,128)} fusion(f32[1,1536]{1,0:T(1,128)S(1)} %get-tuple-element.16, f32[1,1536]{1,0:T(1,128)S(1)} %collective-permute-done.7), kind=kLoop, calls=%fused_computation.2 | loop fusion | flops 1536 | bytes 18432 | tf_op jit(solution)/shard_map/reshape | solution.py:364
  (3 shorter events, 0.0 us)
Async XLA Ops:
  0.6 1.4 %collective-permute-start.3 = (f32[1,1536]{1,0:T(1,128)}, f32[1,1536]{1,0:T(1,128)S(1)}, u32[]{:S(2)}, u32[]{:S(2)}) collective-permute-start(f32[1,1536]{1,0:T(1,128)} %bitcast.18), channel_id=1, source_target_pairs={{0,2},{2,0},{4,6},{6,4},{8,10},{10,8},{12,14},{14,12},{16,18},{18,... | collective-permute-start | bytes 18440 | tf_op jit(solution)/shard_map/ppermute | solution.py:280
  2.1 3.7 %collective-permute-start.4 = (bf16[2,16,128]{2,1,0:T(8,128)(2,1)S(1)}, bf16[2,16,128]{2,1,0:T(8,128)(2,1)S(1)}, u32[]{:S(2)}, u32[]{:S(2)}) collective-permute-start(bf16[2,16,128]{2,1,0:T(8,128)(2,1)S(1)} %shard_map.106), channel_id=1, source_target_pairs={{0,4},{2,6},{4,0},{6,2},{8,12},{10,14},{12,8},{14,10},{16,20},{18,... | collective-permute-start | bytes 24584 | tf_op jit(solution)/shard_map/ppermute | solution.py:306
  5.8 3.7 %collective-permute-start.5 = (bf16[4,16,128]{2,1,0:T(8,128)(2,1)S(1)}, bf16[4,16,128]{2,1,0:T(8,128)(2,1)S(1)}, u32[]{:S(2)}, u32[]{:S(2)}) collective-permute-start(bf16[4,16,128]{2,1,0:T(8,128)(2,1)S(1)} %pad_maximum_fusion.1), channel_id=1, source_target_pairs={{0,8},{2,10},{4,12},{6,14},{8,0},{10,2},{12,4},{14,6},{16,24},{18,... | collective-permute-start | bytes 49160 | tf_op jit(solution)/shard_map/ppermute | solution.py:310
  9.6 13.1 %collective-permute-start.6 = (bf16[8,16,128]{2,1,0:T(8,128)(2,1)S(1)}, bf16[8,16,128]{2,1,0:T(8,128)(2,1)S(1)}, u32[]{:S(2)}, u32[]{:S(2)}) collective-permute-start(bf16[8,16,128]{2,1,0:T(8,128)(2,1)S(1)} %pad_maximum_fusion.mine), channel_id=1, source_target_pairs={{0,16},{2,18},{4,20},{6,22},{8,24},{10,26},{12,28},{14,30},{16,0},... | collective-permute-start | bytes 98312 | tf_op jit(solution)/shard_map/ppermute | solution.py:310
  12.1 4.9 %collective-permute-start.2 = (f32[32,128]{1,0:T(8,128)S(1)}, f32[32,128]{1,0:T(8,128)S(1)}, u32[]{:S(2)}, u32[]{:S(2)}) collective-permute-start(f32[32,128]{1,0:T(8,128)S(1)} %bitcast.16), channel_id=1, source_target_pairs={{0,1},{1,0},{2,3},{3,2},{4,5},{5,4},{6,7},{7,6},{8,9},{9,8},{10,11... | collective-permute-start | bytes 49160 | tf_op jit(solution)/shard_map/ppermute | solution.py:295
  13.7 3.4 %collective-permute-start = (f32[32,128]{1,0:T(8,128)S(1)}, f32[32,128]{1,0:T(8,128)S(1)}, u32[]{:S(2)}, u32[]{:S(2)}) collective-permute-start(f32[32,128]{1,0:T(8,128)S(1)} %get-tuple-element.10), channel_id=1, source_target_pairs={{0,2},{2,0},{4,6},{6,4},{8,10},{10,8},{12,14},{14,12},{16,18},{18,... | collective-permute-start | bytes 49160 | tf_op jit(solution)/shard_map/ppermute | solution.py:293
  13.7 5.9 %collective-permute-start.1 = (f32[32,128]{1,0:T(8,128)S(1)}, f32[32,128]{1,0:T(8,128)S(1)}, u32[]{:S(2)}, u32[]{:S(2)}) collective-permute-start(f32[32,128]{1,0:T(8,128)S(1)} %get-tuple-element.11), channel_id=1, source_target_pairs={{2,4},{6,8},{10,12},{14,16},{18,20},{22,24},{26,28},{4,2},{8,6},{1... | collective-permute-start | bytes 49160 | tf_op jit(solution)/shard_map/ppermute | solution.py:294
  19.6 3.0 %copy-start = (bf16[16,16,1,1536]{3,1,2,0:T(8,128)(2,1)S(1)}, bf16[16,16,1,1536]{3,1,2,0:T(8,128)(2,1)}, u32[]{:S(2)}) copy-start(bf16[16,16,1,1536]{3,1,2,0:T(8,128)(2,1)} %param.17) | copy-start | bytes 2359300
  19.6 3.0 %copy-start.1 = (bf16[16,1,2,1536]{3,2,1,0:T(2,128)(2,1)S(1)}, bf16[16,1,2,1536]{3,2,1,0:T(2,128)(2,1)}, u32[]{:S(2)}) copy-start(bf16[16,1,2,1536]{3,2,1,0:T(2,128)(2,1)} %param.16) | copy-start | bytes 294916
  23.1 3.7 %collective-permute-start.7 = (f32[1,1536]{1,0:T(1,128)S(1)}, f32[1,1536]{1,0:T(1,128)S(1)}, u32[]{:S(2)}, u32[]{:S(2)}) collective-permute-start(f32[1,1536]{1,0:T(1,128)S(1)} %bitcast.17), channel_id=1, source_target_pairs={{0,1},{1,0},{2,3},{3,2},{4,5},{5,4},{6,7},{7,6},{8,9},{9,8},{10,11... | collective-permute-start | bytes 18440 | tf_op jit(solution)/shard_map/ppermute | solution.py:363

commit v3 on v2

--- a/solution.py
+++ b/solution.py
@@ -8,6 +8,7 @@
 from jax.sharding import PartitionSpec as P
 
 LANES = 128
+COST = 10**10
 NT = (((1,), (1,)), ((), ()))
 
 
@@ -31,6 +32,7 @@
         copies.append(pltpu.make_async_copy(source, target, sems.at[len(copies)]))
         copies[-1].start()
 
+    copy(boundary, boundary_out)
     for slot, comp in enumerate((1, 2)):
         rows = pl.ds(slot * cells_y, cells_y)
         copy(field.at[comp, inner], inner_out.at[rows])
@@ -40,65 +42,25 @@
         for slot, comp in enumerate((0, 2)):
             rows = pl.ds(slot * cells_x, cells_x)
             copy(field.at[comp, :, row], y_out.at[side, rows])
-    copy(boundary, boundary_out)
     for one in copies:
         one.wait()
 
 
 def pack_kernel(mine, theirs, out):
-    rows = mine.shape[1] // LANES
-    for i, source in enumerate((mine, theirs)):
-        lines = [source[:, q * LANES : (q + 1) * LANES] for q in range(rows)]
-        lines.append(jnp.zeros((out.shape[1] - rows, LANES), jnp.float32))
-        out[i] = jnp.concatenate(lines, axis=0).astype(jnp.bfloat16)
-
-
-def volume_kernel(
-    x_index,
-    y_index,
-    field_in,
-    diag_in,
-    face_in,
-    boundary_in,
-    self_in,
-    coupling_in,
-    owner_in,
-    x_inner,
-    x_outer,
-    y_halo,
-    volume_out,
-    base_out,
-    field,
-    diag,
-    face,
-    boundary,
-    self_term,
-    coupling,
-    owner,
-    sems,
-):
-    pairs = (
-        (owner_in, owner),
-        (coupling_in, coupling),
-        (boundary_in, boundary),
-        (self_in, self_term),
-        (field_in, field),
-        (diag_in, diag),
-        (face_in, face),
-    )
-    loads = [pltpu.make_async_copy(a, b, sems.at[i]) for i, (a, b) in enumerate(pairs)]
-    for load in loads:
-        load.start()
-    _, cells_x, cells_y, cells_z = field.shape
+    lines = [
+        source[:, q * LANES : (q + 1) * LANES]
+        for source in (mine, theirs)
+        for q in range(mine.shape[1] // LANES)
+    ]
+    out[...] = jnp.concatenate(lines, axis=0).astype(jnp.bfloat16)
+
+
+def prepare_kernel(field, boundary, self_term, coupling, owner, placed_out, base_out):
+    _, _, _, cells_z = field.shape
     count = boundary.shape[1]
     blocks = count // LANES
     half = blocks // 2
     padded = -(-blocks // 16) * 16
-    even_x = x_index[0] % 2 == 0
-    even_y = y_index[0] % 2 == 0
-
-    for load in loads[:4]:
-        load.wait()
 
     slot_of = owner[...]
     lane_of = slot_of % LANES
@@ -111,43 +73,56 @@
     in_block = block_of == lax.broadcasted_iota(jnp.int32, (padded, count), 0)
 
     spread = jnp.where(in_block, coupling[...] * boundary[...], 0.0)
-    placed = jnp.zeros((LANES, padded), jnp.float32)
-    for term in split3(spread):
-        placed += lax.dot_general(onehot, term, NT, preferred_element_type=jnp.float32)
-
-    ends = lax.broadcasted_iota(jnp.int32, (16, cells_z), 0)
-    lane = lax.broadcasted_iota(jnp.int32, (16, cells_z), 1)
-    pick = (
-        (((ends == 0) & (lane == 0)) | ((ends == 1) & (lane == cells_z - 1)))
-        .astype(jnp.float32)
-        .astype(jnp.bfloat16)
-    )
-    loads[4].wait()
-    flat = field[...].reshape(3 * cells_x * cells_y, cells_z)
-    surface = jnp.zeros((16, 3 * cells_x * cells_y), jnp.float32)
-    for term in split3(flat):
-        surface += lax.dot_general(pick, term, NT, preferred_element_type=jnp.float32)
-    table = jnp.concatenate(
-        [
-            surface[e : e + 1, b * LANES : (b + 1) * LANES]
-            for e in range(2)
-            for b in range(half)
-        ]
-        + [jnp.zeros((padded - blocks, LANES), jnp.float32)],
-        axis=0,
-    )
-    read = jnp.zeros((padded, count), jnp.float32)
-    for term in split3(table):
-        read += jnp.dot(term, onehot, preferred_element_type=jnp.float32)
+    terms = jnp.concatenate(split3(spread), axis=0)
+    placed = lax.dot_general(onehot, terms, NT, preferred_element_type=jnp.float32)
+    placed_out[...] = (
+        placed[:, :padded] + placed[:, padded : 2 * padded] + placed[:, 2 * padded :]
+    )
+
+    terms, picks = [], []
+    lane = lax.broadcasted_iota(jnp.int32, (cells_z, padded), 1)
+    level = lax.broadcasted_iota(jnp.int32, (cells_z, padded), 0)
+    flat = field[...].reshape(half, LANES, cells_z)
+    for b in range(half):
+        chosen = ((level == 0) & (lane == b)) | ((level == cells_z - 1) & (lane == half + b))
+        terms += split3(flat[b])
+        picks += [chosen.astype(jnp.float32).astype(jnp.bfloat16)] * 3
+    table = jnp.dot(
+        jnp.concatenate(terms, axis=1),
+        jnp.concatenate(picks, axis=0),
+        preferred_element_type=jnp.float32,
+    )
+    table = jnp.concatenate(split3(table.T), axis=0)
+    read = jnp.dot(table, onehot, preferred_element_type=jnp.float32)
+    read = read[:padded] + read[padded : 2 * padded] + read[2 * padded :]
     trace = jnp.sum(jnp.where(in_block, read, 0.0), axis=0, keepdims=True)
     base_out[...] = self_term[...] * boundary[...] + coupling[...] * trace
 
-    for load in loads[5:]:
-        load.wait()
+
+def stencil_kernel(
+    x_index,
+    y_index,
+    field,
+    diag,
+    face,
+    x_inner,
+    x_outer,
+    y_halo,
+    placed,
+    volume_out,
+    result,
+    sems,
+):
+    _, cells_x, cells_y, cells_z = field.shape
+    half = 3 * cells_x * cells_y // LANES
+    chunk = cells_x // sems.shape[0]
+    even_x = x_index[0] % 2 == 0
+    even_y = y_index[0] % 2 == 0
     z_at = lax.broadcasted_iota(jnp.int32, (cells_y, cells_z), 1)
     y_at = lax.broadcasted_iota(jnp.int32, (cells_y, cells_z), 0)
     first_z, last_z = z_at == 0, z_at == cells_z - 1
     first_y, last_y = y_at == 0, y_at == cells_y - 1
+    stores = []
     for x in range(cells_x):
         own = [field[c, x] for c in range(3)]
         x_plus, x_minus = {}, {}
@@ -196,23 +171,37 @@
             total[comp] = total[comp] + jnp.where(
                 first_z, bottom, jnp.where(last_z, top, 0.0)
             )
-            volume_out[comp, x] = total[comp]
-
-
-def integral_kernel(x_index, y_index, mine, theirs, right, left, base, own_out, send_out, stack, partial_value):
+            result[comp, x] = total[comp]
+        if (x + 1) % chunk == 0:
+            part = pl.ds(x + 1 - chunk, chunk)
+            stores.append(
+                pltpu.make_async_copy(
+                    result.at[:, part], volume_out.at[:, part], sems.at[len(stores)]
+                )
+            )
+            stores[-1].start()
+    for store in stores:
+        store.wait()
+
+
+def integral_kernel(
+    steps, x_index, y_index, mine, theirs, right, left, own_out, send_out, stack, partial_value
+):
     columns = left.shape[1]
-    rank, groups = right.shape[0], right.shape[1]
-    count = right.shape[2]
+    rank, groups, count = right.shape
+    pitch = count // LANES
     held = mine.shape[0]
-    pitch = mine.shape[1]
-    stack[0 : held * pitch, :] = mine[...].astype(jnp.float32).reshape(held * pitch, LANES)
-    stack[held * pitch :, :] = theirs[...].astype(jnp.float32).reshape(held * pitch, LANES)
-    pieces = [stack[pl.ds(q, groups, stride=pitch), :] for q in range(count // LANES)]
+    stack[0:held, :] = mine[...].astype(jnp.float32)
+    stack[held:, :] = theirs[...].astype(jnp.float32)
+    pieces = [stack[pl.ds(q, groups, stride=pitch), :] for q in range(pitch)]
     gathered = jnp.concatenate(pieces, axis=1).astype(jnp.bfloat16)
     table = right[...].reshape(rank * groups, count)
     product = lax.dot_general(table, gathered, NT, preferred_element_type=jnp.float32)
     product = product.reshape(rank, groups, groups)
-    source = lax.broadcasted_iota(jnp.int32, (rank, groups, groups), 2) ^ x_index[0]
+    block = lax.broadcasted_iota(jnp.int32, (rank, groups, groups), 2)
+    source = jnp.full((rank, groups, groups), x_index[0], jnp.int32)
+    for bit, step in enumerate(steps):
+        source = source ^ (((block >> bit) & 1) * step)
     group = lax.broadcasted_iota(jnp.int32, (rank, groups, groups), 1)
     product = jnp.where(source == group, product, 0.0)
     coef = jnp.sum(jnp.sum(product, axis=1, keepdims=True), axis=2, keepdims=True)
@@ -222,7 +211,7 @@
         total = total + coef[r] * left[r].astype(jnp.float32)
     partial_value[...] = total
     me = y_index[0]
-    own_out[...] = base[...] + partial_value[pl.ds(me, 1), :]
+    own_out[...] = partial_value[pl.ds(me, 1), :]
     for step in range(1, columns):
         to = lax.rem(me + step, columns)
         send_out[step - 1] = partial_value[pl.ds(to, 1), :]
@@ -246,6 +235,7 @@
     count = boundary_field.shape[2]
     rank = left_basis.shape[0]
     rows = count // LANES
+    row = (1, count)
     head = -(-rows // 16) * 16
     x_index = lax.axis_index("gx").reshape(1)
     y_index = lax.axis_index("gy").reshape(1)
@@ -255,7 +245,7 @@
     hbm = pl.BlockSpec(memory_space=pltpu.HBM)
     y_sides = 1 if n_y == 2 else 2
 
-    def call(body, outs, args, scratch=(), far=0, indices=True):
+    def call(body, outs, args, scratch=(), far=0, indices=True, far_outs=0, cost=0):
         lead = (x_index, y_index) if indices else ()
         args = [
             pltpu.with_memory_space_constraint(arg, pltpu.HBM if i < far else pltpu.VMEM)
@@ -265,9 +255,10 @@
             body,
             out_shape=outs,
             in_specs=[smem] * len(lead) + [hbm] * far + [vmem] * (len(args) - far),
-            out_specs=[vmem] * len(outs),
+            out_specs=[hbm] * far_outs + [vmem] * (len(outs) - far_outs),
             scratch_shapes=scratch,
             compiler_params=pltpu.CompilerParams(vmem_limit_bytes=16 * 2**20),
+            cost_estimate=pl.CostEstimate(flops=cost, transcendentals=0, bytes_accessed=0),
         )(*lead, *args)
 
     def inner_pairs(size):
@@ -284,11 +275,12 @@
             pltpu.VMEM((2 * cells_y, LANES), f32),
             pltpu.VMEM((2 * cells_y, LANES), f32),
             pltpu.VMEM((y_sides, 2 * cells_x, LANES), f32),
-            pltpu.VMEM((1, count), f32),
+            pltpu.VMEM(row, f32),
         ],
         [volume_field, boundary],
         [pltpu.SemaphoreType.DMA((5 + 2 * y_sides,))],
         far=2,
+        cost=COST,
     )
     x_inner = lax.ppermute(inner_pay, "gx", inner_pairs(n_x))
     x_outer = lax.ppermute(outer_pay, "gx", outer_pairs(n_x))
@@ -299,65 +291,59 @@
 
     (mine,) = call(
         pack_kernel,
-        [pltpu.VMEM((2, head, LANES), jnp.bfloat16)],
+        [pltpu.VMEM((2 * rows, LANES), jnp.bfloat16)],
         [near_boundary, core_got],
         indices=False,
     )
-    theirs = lax.ppermute(mine, "gx", [(i, i ^ 2) for i in range(n_x)])
-    step = 4
+    steps = [1]
+    step = 2
     while step < n_x:
-        mine = jnp.concatenate([mine, theirs], axis=0)
-        theirs = lax.ppermute(mine, "gx", [(i, i ^ step) for i in range(n_x)])
+        steps.append(step)
+        pairs = [(i, i ^ step) for i in range(n_x)]
+        theirs = lax.ppermute(mine, "gx", pairs)
+        if 2 * step < n_x:
+            mine = jnp.concatenate([mine, theirs], axis=0)
         step *= 2
 
-    row = (1, count)
-    volume_out, base = call(
-        volume_kernel,
-        [pltpu.VMEM(volume_field.shape, f32), pltpu.VMEM(row, f32)],
+    placed, base = call(
+        prepare_kernel,
+        [pltpu.VMEM((LANES, head), f32), pltpu.VMEM(row, f32)],
         [
             volume_field,
-            diag_blocks,
-            face_weights,
-            boundary,
+            near_boundary,
             self_term.reshape(row),
             coupling.reshape(row),
             owner_map.reshape(row),
-            x_inner,
-            x_outer,
-            y_halo,
         ],
-        [
-            pltpu.VMEM(volume_field.shape, f32),
-            pltpu.VMEM(diag_blocks.shape, f32),
-            pltpu.VMEM(face_weights.shape, f32),
-            pltpu.VMEM(row, f32),
-            pltpu.VMEM(row, f32),
-            pltpu.VMEM(row, f32),
-            pltpu.VMEM(row, jnp.int32),
-            pltpu.SemaphoreType.DMA((7,)),
-        ],
-        far=7,
+        indices=False,
+        cost=COST,
     )
 
     own, shares = call(
-        integral_kernel,
-        [
-            pltpu.VMEM((1, count), f32),
-            pltpu.VMEM((n_y - 1, 1, count), f32),
-        ],
+        functools.partial(integral_kernel, tuple(steps)),
+        [pltpu.VMEM(row, f32), pltpu.VMEM((n_y - 1, 1, count), f32)],
         [
             mine,
             theirs,
             right_basis.reshape(rank, n_x, count),
             left_basis.reshape(rank, n_y, count),
-            base,
         ],
         [
-            pltpu.VMEM((n_x * head, LANES), f32),
+            pltpu.VMEM((n_x * rows, LANES), f32),
             pltpu.VMEM((n_y, count), f32),
         ],
-    )
-    total = own
+        cost=COST,
+    )
+
+    (volume_out,) = call(
+        stencil_kernel,
+        [jax.ShapeDtypeStruct(volume_field.shape, f32)],
+        [volume_field, diag_blocks, face_weights, x_inner, x_outer, y_halo, placed],
+        [pltpu.VMEM(volume_field.shape, f32), pltpu.SemaphoreType.DMA((4,))],
+        far_outs=1,
+        cost=COST,
+    )
+    total = base + own
     for shift in range(1, n_y):
         pairs = [(i, (i + shift) % n_y) for i in range(n_y)]
         total = total + lax.ppermute(shares[shift - 1], "gy", pairs)

time: 27.7 us -> 22 us (0.79)
  the two profiles are of different devices: /device:TPU:8 before, /device:TPU:0 now
where the time goes in v3:
time: 22 us; the launch traced here: 21.9 us
  starting transfers between devices  12.6 us (57%)
  waiting for transfers between devices  3.94 us (18%)
  Pallas kernels  3.32 us (15%)
  local copies, waits for them, and re-layouts  0.74 us (3%)
  between operations  0.71 us (3%)
  other arithmetic  0.61 us (3%)
    ppermute x3, starting transfers between devices, on_device(): theirs = lax.ppermute(mine, 'gx', pairs)  9.19 us
    pallas_call x5, Pallas kernels, call(): pl.pallas_call(body, out_shape=outs, in_specs=[smem] * len(lead) + [hbm]...  3.32 us
    ppermute x3, waiting for transfers between devices, on_device(): theirs = lax.ppermute(mine, 'gx', pairs)  2.7 us
    ppermute x1, starting transfers between devices, on_device(): y_halo = lax.ppermute(y_pay[0], 'gy', inner_pairs(n_y))[None]  1.58 us
    ppermute x1, waiting for transfers between devices, on_device(): total = total + lax.ppermute(shares[shift - 1], 'gy', pairs)  1.12 us
    unnamed x16, local copies, waits for them, and re-layouts  0.74 us
    ppermute x1, starting transfers between devices, on_device(): x_outer = lax.ppermute(outer_pay, 'gx', outer_pairs(n_x))  0.65 us
    reshape x1, other arithmetic, on_device(): return (volume_out, total.reshape(boundary_field.shape))  0.6 us
  transfers between devices with their start and end apart: 8, of which 4 were waited for; matrix products, arithmetic and copies ran while one was open for 0% of the time, Pallas kernels for 15%

profile of v3, /device:TPU:0, one launch (start us, length us, event | category | flops | bytes accessed | tf_op | source)
XLA Modules:
  0.0 21.9 jit_solution(125517873321455311)
XLA Ops:
  0.6 0.6 %collective-permute-start.3 = (f32[1,1536]{1,0:T(1,128)}, f32[1,1536]{1,0:T(1,128)S(1)}, u32[]{:S(2)}, u32[]{:S(2)}) collective-permute-start(f32[1,1536]{1,0:T(1,128)} %bitcast.21), channel_id=1, source_target_pairs={{0,2},{2,0},{4,6},{6,4},{8,10},{10,8},{12,14},{14,12},{16,18},{18,... | collective-permute-start | bytes 18440 | tf_op jit(solution)/shard_map/ppermute | solution.py:271
  1.2 0.0 copy-start.3
  1.2 0.0 copy-start.5
  1.2 0.0 copy-start.6
  1.2 0.0 copy-start.7
  1.2 0.9 %shard_map.104 = (f32[32,128]{1,0:T(8,128)S(1)}, f32[32,128]{1,0:T(8,128)S(1)}, f32[1,32,128]{2,1,0:T(8,128)S(1)}, f32[1,1536]{1,0:T(1,128)S(1)}) custom-call(s32[1]{0:T(128)} %bitcast.x_index, s32[1]{0:T(128)} %bitcast.1.y_index, f32[3,16,16,128]{3,2,1,0:T(8,128)} %field.5, f32[1,1536]{1,0:T(1,128)} %bitcast.22), custom_call_target="tpu_custom_call" | custom-call | flops 10000000000 | tf_op jit(solution)/shard_map/pallas_call | solution.py:254
  2.1 0.1 collective-permute-done.3.theirs
  2.2 2.9 %collective-permute-start.4 = (bf16[24,128]{1,0:T(8,128)(2,1)S(1)}, bf16[24,128]{1,0:T(8,128)(2,1)S(1)}, u32[]{:S(2)}, u32[]{:S(2)}) collective-permute-start(bf16[24,128]{1,0:T(8,128)(2,1)S(1)} %shard_map.107), channel_id=1, source_target_pairs={{0,4},{2,6},{4,0},{6,2},{8,12},{10,14},{12,8},{14,10},{16,20},{18,... | collective-permute-start | bytes 18440 | tf_op jit(solution)/shard_map/ppermute | solution.py:303
  5.1 1.6 %collective-permute-done.4 = bf16[24,128]{1,0:T(8,128)(2,1)S(1)} collective-permute-done((bf16[24,128]{1,0:T(8,128)(2,1)S(1)}, bf16[24,128]{1,0:T(8,128)(2,1)S(1)}, u32[]{:S(2)}, u32[]{:S(2)}) %collective-permute-start.4) | collective-permute-done | bytes 6176 | tf_op jit(solution)/shard_map/ppermute | solution.py:303
  6.7 2.1 %collective-permute-start.5 = (bf16[48,128]{1,0:T(8,128)(2,1)S(1)}, bf16[48,128]{1,0:T(8,128)(2,1)S(1)}, u32[]{:S(2)}, u32[]{:S(2)}) collective-permute-start(bf16[48,128]{1,0:T(8,128)(2,1)S(1)} %pad_maximum_fusion.1), channel_id=1, source_target_pairs={{0,8},{2,10},{4,12},{6,14},{8,0},{10,2},{12,4},{14,6},{16,24},{18,... | collective-permute-start | bytes 36872 | tf_op jit(solution)/shard_map/ppermute | solution.py:303
  8.8 0.0 collective-permute-start
  8.8 0.7 %collective-permute-start.1 = (f32[32,128]{1,0:T(8,128)S(1)}, f32[32,128]{1,0:T(8,128)S(1)}, u32[]{:S(2)}, u32[]{:S(2)}) collective-permute-start(f32[32,128]{1,0:T(8,128)S(1)} %get-tuple-element.11), channel_id=1, source_target_pairs={{2,4},{6,8},{10,12},{14,16},{18,20},{22,24},{26,28},{4,2},{8,6},{1... | collective-permute-start | bytes 49160 | tf_op jit(solution)/shard_map/ppermute | solution.py:286
  9.5 1.6 %collective-permute-start.2 = (f32[32,128]{1,0:T(8,128)S(1)}, f32[32,128]{1,0:T(8,128)S(1)}, u32[]{:S(2)}, u32[]{:S(2)}) collective-permute-start(f32[32,128]{1,0:T(8,128)S(1)} %bitcast.15), channel_id=1, source_target_pairs={{0,1},{1,0},{2,3},{3,2},{4,5},{5,4},{6,7},{7,6},{8,9},{9,8},{10,11... | collective-permute-start | bytes 49160 | tf_op jit(solution)/shard_map/ppermute | solution.py:287
  11.1 0.0 collective-permute-done.5
  11.1 4.2 %collective-permute-start.6 = (bf16[96,128]{1,0:T(8,128)(2,1)S(1)}, bf16[96,128]{1,0:T(8,128)(2,1)S(1)}, u32[]{:S(2)}, u32[]{:S(2)}) collective-permute-start(bf16[96,128]{1,0:T(8,128)(2,1)S(1)} %pad_maximum_fusion.mine), channel_id=1, source_target_pairs={{0,16},{2,18},{4,20},{6,22},{8,24},{10,26},{12,28},{14,30},{16,0},... | collective-permute-start | bytes 73736 | tf_op jit(solution)/shard_map/ppermute | solution.py:303
  15.3 0.0 copy-done.3
  15.3 0.0 copy-done.5
  15.3 0.0 copy-done.6
  15.3 0.0 copy-done.7
  15.3 0.0 copy-start.2
  15.3 0.0 copy-start.4
  15.3 0.7 %shard_map.105 = (f32[128,16]{1,0:T(8,128)S(1)}, f32[1,1536]{1,0:T(1,128)S(1)}) custom-call(f32[3,16,16,128]{3,2,1,0:T(8,128)S(1)} %copy-done.3, f32[1,1536]{1,0:T(1,128)S(1)} %get-tuple-element.13.boundary.mine, f32[1,1536]{1,0:T(1,128)S(1)} %bitcast.17, f32[1,1536]{1,0:T(1,128)S(1)} %bitcast.18, s32[1,1536]{1,0:T(1,128)S(1)} %bitcast.19), custom_call_target="tpu_custom_call" | custom-call | flops 10000000000 | tf_op jit(solution)/shard_map/pallas_call | solution.py:254
  16.0 1.1 %collective-permute-done.6.theirs = bf16[96,128]{1,0:T(8,128)(2,1)S(1)} collective-permute-done((bf16[96,128]{1,0:T(8,128)(2,1)S(1)}, bf16[96,128]{1,0:T(8,128)(2,1)S(1)}, u32[]{:S(2)}, u32[]{:S(2)}) %collective-permute-start.6) | collective-permute-done | bytes 24608 | tf_op jit(solution)/shard_map/ppermute | solution.py:303
  17.1 0.0 copy-done.2
  17.1 0.0 copy-done.4
  17.1 0.0 copy-start
  17.1 0.0 copy-start.1
  17.1 0.4 %shard_map.108 = (f32[1,1536]{1,0:T(1,128)S(1)}, f32[1,1,1536]{2,1,0:T(1,128)S(1)}) custom-call(s32[1]{0:T(128)} %bitcast.x_index, s32[1]{0:T(128)} %bitcast.1.y_index, bf16[96,128]{1,0:T(8,128)(2,1)S(1)} %pad_maximum_fusion.mine, bf16[96,128]{1,0:T(8,128)(2,1)S(1)} %collective-permute-done.6.theirs, bf16[16,16,1536]{2,1,0:T(8,128)(2,1)S(1)} %bitcast.13, ...), custom_call_target="tpu_custom_call" | custom-call | flops 10000000000 | tf_op jit(solution)/shard_map/pallas_call | solution.py:254
  17.6 0.6 %collective-permute-start.7 = (f32[1,1536]{1,0:T(1,128)S(1)}, f32[1,1536]{1,0:T(1,128)S(1)}, u32[]{:S(2)}, u32[]{:S(2)}) collective-permute-start(f32[1,1536]{1,0:T(1,128)S(1)} %bitcast.20), channel_id=1, source_target_pairs={{0,1},{1,0},{2,3},{3,2},{4,5},{5,4},{6,7},{7,6},{8,9},{9,8},{10,11... | collective-permute-start | bytes 18440 | tf_op jit(solution)/shard_map/ppermute | solution.py:349
  18.1 0.0 collective-permute-done.x_inner
  18.1 0.0 collective-permute-done.1.x_outer
  18.1 0.0 collective-permute-done.2
  18.2 0.4 %copy-done = f32[6,2,16,16,128]{4,3,2,1,0:T(8,128)S(1)} copy-done((f32[6,2,16,16,128]{4,3,2,1,0:T(8,128)S(1)}, f32[6,2,16,16,128]{4,3,2,1,0:T(8,128)}, u32[]{:S(2)}) %copy-start) | copy-done | bytes 1572888
  18.5 0.3 %copy-done.1 = f32[3,3,16,16,128]{4,3,2,1,0:T(8,128)S(1)} copy-done((f32[3,3,16,16,128]{4,3,2,1,0:T(8,128)S(1)}, f32[3,3,16,16,128]{4,3,2,1,0:T(8,128)}, u32[]{:S(2)}) %copy-start.1) | copy-done | bytes 1179672
  18.9 1.3 %shard_map.106 = f32[3,16,16,128]{3,2,1,0:T(8,128)} custom-call(s32[1]{0:T(128)} %bitcast.x_index, s32[1]{0:T(128)} %bitcast.1.y_index, f32[3,16,16,128]{3,2,1,0:T(8,128)S(1)} %copy-done.3, f32[3,3,16,16,128]{4,3,2,1,0:T(8,128)S(1)} %copy-done.1, f32[6,2,16,16,128]{4,3,2,1,0:T(8,128)S(1)} %copy-done, f32[32,128]{1,0:T(8,128)S(1)} %collective-permute-done.x_inner, ...), custom_call_target="tpu_custom_call" | custom-call | flops 10000000000 | tf_op jit(solution)/shard_map/pallas_call | solution.py:254
  20.1 1.1 %collective-permute-done.7 = f32[1,1536]{1,0:T(1,128)S(1)} collective-permute-done((f32[1,1536]{1,0:T(1,128)S(1)}, f32[1,1536]{1,0:T(1,128)S(1)}, u32[]{:S(2)}, u32[]{:S(2)}) %collective-permute-start.7) | collective-permute-done | bytes 6176 | tf_op jit(solution)/shard_map/ppermute | solution.py:349
  21.3 0.6 %add_bitcast_fusion = f32[1,1,1536]{2,1,0:T(1,128)} fusion(f32[1,1536]{1,0:T(1,128)S(1)} %collective-permute-done.7, f32[1,1536]{1,0:T(1,128)S(1)} %get-tuple-element.15, f32[1,1536]{1,0:T(1,128)S(1)} %get-tuple-element.16), kind=kLoop, calls=%fused_computation.2 | loop fusion | flops 3072 | bytes 24576 | tf_op jit(solution)/shard_map/reshape | solution.py:350
  (3 shorter events, 0.0 us)
Async XLA Ops:
  0.6 1.6 %collective-permute-start.3 = (f32[1,1536]{1,0:T(1,128)}, f32[1,1536]{1,0:T(1,128)S(1)}, u32[]{:S(2)}, u32[]{:S(2)}) collective-permute-start(f32[1,1536]{1,0:T(1,128)} %bitcast.21), channel_id=1, source_target_pairs={{0,2},{2,0},{4,6},{6,4},{8,10},{10,8},{12,14},{14,12},{16,18},{18,... | collective-permute-start | bytes 18440 | tf_op jit(solution)/shard_map/ppermute | solution.py:271
  1.2 14.1 %copy-start.3 = (f32[3,16,16,128]{3,2,1,0:T(8,128)S(1)}, f32[3,16,16,128]{3,2,1,0:T(8,128)}, u32[]{:S(2)}) copy-start(f32[3,16,16,128]{3,2,1,0:T(8,128)} %field.5) | copy-start | bytes 1179652
  1.2 14.1 %copy-start.5 = (f32[1,1,1536]{2,1,0:T(1,128)S(1)}, f32[1,1,1536]{2,1,0:T(1,128)}, u32[]{:S(2)}) copy-start(f32[1,1,1536]{2,1,0:T(1,128)} %param.13) | copy-start | bytes 18436
  1.2 14.1 %copy-start.6 = (f32[1,1,1536]{2,1,0:T(1,128)S(1)}, f32[1,1,1536]{2,1,0:T(1,128)}, u32[]{:S(2)}) copy-start(f32[1,1,1536]{2,1,0:T(1,128)} %param.14) | copy-start | bytes 18436
  1.2 14.1 %copy-start.7 = (s32[1,1,1536]{2,1,0:T(1,128)S(1)}, s32[1,1,1536]{2,1,0:T(1,128)}, u32[]{:S(2)}) copy-start(s32[1,1,1536]{2,1,0:T(1,128)} %param.15) | copy-start | bytes 18436
  2.2 4.5 %collective-permute-start.4 = (bf16[24,128]{1,0:T(8,128)(2,1)S(1)}, bf16[24,128]{1,0:T(8,128)(2,1)S(1)}, u32[]{:S(2)}, u32[]{:S(2)}) collective-permute-start(bf16[24,128]{1,0:T(8,128)(2,1)S(1)} %shard_map.107), channel_id=1, source_target_pairs={{0,4},{2,6},{4,0},{6,2},{8,12},{10,14},{12,8},{14,10},{16,20},{18,... | collective-permute-start | bytes 18440 | tf_op jit(solution)/shard_map/ppermute | solution.py:303
  6.7 4.4 %collective-permute-start.5 = (bf16[48,128]{1,0:T(8,128)(2,1)S(1)}, bf16[48,128]{1,0:T(8,128)(2,1)S(1)}, u32[]{:S(2)}, u32[]{:S(2)}) collective-permute-start(bf16[48,128]{1,0:T(8,128)(2,1)S(1)} %pad_maximum_fusion.1), channel_id=1, source_target_pairs={{0,8},{2,10},{4,12},{6,14},{8,0},{10,2},{12,4},{14,6},{16,24},{18,... | collective-permute-start | bytes 36872 | tf_op jit(solution)/shard_map/ppermute | solution.py:303
  8.8 9.3 %collective-permute-start = (f32[32,128]{1,0:T(8,128)S(1)}, f32[32,128]{1,0:T(8,128)S(1)}, u32[]{:S(2)}, u32[]{:S(2)}) collective-permute-start(f32[32,128]{1,0:T(8,128)S(1)} %get-tuple-element.10), channel_id=1, source_target_pairs={{0,2},{2,0},{4,6},{6,4},{8,10},{10,8},{12,14},{14,12},{16,18},{18,... | collective-permute-start | bytes 49160 | tf_op jit(solution)/shard_map/ppermute | solution.py:285
  8.8 9.3 %collective-permute-start.1 = (f32[32,128]{1,0:T(8,128)S(1)}, f32[32,128]{1,0:T(8,128)S(1)}, u32[]{:S(2)}, u32[]{:S(2)}) collective-permute-start(f32[32,128]{1,0:T(8,128)S(1)} %get-tuple-element.11), channel_id=1, source_target_pairs={{2,4},{6,8},{10,12},{14,16},{18,20},{22,24},{26,28},{4,2},{8,6},{1... | collective-permute-start | bytes 49160 | tf_op jit(solution)/shard_map/ppermute | solution.py:286
  9.5 8.6 %collective-permute-start.2 = (f32[32,128]{1,0:T(8,128)S(1)}, f32[32,128]{1,0:T(8,128)S(1)}, u32[]{:S(2)}, u32[]{:S(2)}) collective-permute-start(f32[32,128]{1,0:T(8,128)S(1)} %bitcast.15), channel_id=1, source_target_pairs={{0,1},{1,0},{2,3},{3,2},{4,5},{5,4},{6,7},{7,6},{8,9},{9,8},{10,11... | collective-permute-start | bytes 49160 | tf_op jit(solution)/shard_map/ppermute | solution.py:287
  11.1 6.0 %collective-permute-start.6 = (bf16[96,128]{1,0:T(8,128)(2,1)S(1)}, bf16[96,128]{1,0:T(8,128)(2,1)S(1)}, u32[]{:S(2)}, u32[]{:S(2)}) collective-permute-start(bf16[96,128]{1,0:T(8,128)(2,1)S(1)} %pad_maximum_fusion.mine), channel_id=1, source_target_pairs={{0,16},{2,18},{4,20},{6,22},{8,24},{10,26},{12,28},{14,30},{16,0},... | collective-permute-start | bytes 73736 | tf_op jit(solution)/shard_map/ppermute | solution.py:303
  15.3 1.8 %copy-start.2 = (bf16[16,16,1,1536]{3,1,2,0:T(8,128)(2,1)S(1)}, bf16[16,16,1,1536]{3,1,2,0:T(8,128)(2,1)}, u32[]{:S(2)}) copy-start(bf16[16,16,1,1536]{3,1,2,0:T(8,128)(2,1)} %param.17) | copy-start | bytes 2359300
  15.3 1.8 %copy-start.4 = (bf16[16,1,2,1536]{3,2,1,0:T(2,128)(2,1)S(1)}, bf16[16,1,2,1536]{3,2,1,0:T(2,128)(2,1)}, u32[]{:S(2)}) copy-start(bf16[16,1,2,1536]{3,2,1,0:T(2,128)(2,1)} %param.16) | copy-start | bytes 294916
  17.1 1.4 %copy-start = (f32[6,2,16,16,128]{4,3,2,1,0:T(8,128)S(1)}, f32[6,2,16,16,128]{4,3,2,1,0:T(8,128)}, u32[]{:S(2)}) copy-start(f32[6,2,16,16,128]{4,3,2,1,0:T(8,128)} %face.1) | copy-start | bytes 4718596
  17.1 1.7 %copy-start.1 = (f32[3,3,16,16,128]{4,3,2,1,0:T(8,128)S(1)}, f32[3,3,16,16,128]{4,3,2,1,0:T(8,128)}, u32[]{:S(2)}) copy-start(f32[3,3,16,16,128]{4,3,2,1,0:T(8,128)} %diag.1) | copy-start | bytes 3538948
  17.6 3.7 %collective-permute-start.7 = (f32[1,1536]{1,0:T(1,128)S(1)}, f32[1,1536]{1,0:T(1,128)S(1)}, u32[]{:S(2)}, u32[]{:S(2)}) collective-permute-start(f32[1,1536]{1,0:T(1,128)S(1)} %bitcast.20), channel_id=1, source_target_pairs={{0,1},{1,0},{2,3},{3,2},{4,5},{5,4},{6,7},{7,6},{8,9},{9,8},{10,11... | collective-permute-start | bytes 18440 | tf_op jit(solution)/shard_map/ppermute | solution.py:349

commit v4 on v3

--- a/solution.py
+++ b/solution.py
@@ -21,10 +21,10 @@
 
 
 def halo_kernel(
-    x_index, y_index, field, boundary, inner_out, outer_out, y_out, boundary_out, sems
+    x_index, y_index, field, boundary, inner_out, outer_out, y_out, boundary_out, inner, sems
 ):
     cells_x, cells_y = field.shape[1], field.shape[2]
-    inner = jnp.where(x_index[0] % 2 == 0, cells_x - 1, 0)
+    at_inner = jnp.where(x_index[0] % 2 == 0, cells_x - 1, 0)
     beside = jnp.where(y_index[0] % 2 == 0, cells_y - 1, 0)
     copies = []
 
@@ -35,8 +35,8 @@
     copy(boundary, boundary_out)
     for slot, comp in enumerate((1, 2)):
         rows = pl.ds(slot * cells_y, cells_y)
-        copy(field.at[comp, inner], inner_out.at[rows])
-        copy(field.at[comp, cells_x - 1 - inner], outer_out.at[rows])
+        copy(field.at[comp, at_inner], inner.at[rows])
+        copy(field.at[comp, cells_x - 1 - at_inner], outer_out.at[rows])
     for side in range(y_out.shape[0]):
         row = beside if side == 0 else cells_y - 1 - beside
         for slot, comp in enumerate((0, 2)):
@@ -44,6 +44,7 @@
             copy(field.at[comp, :, row], y_out.at[side, rows])
     for one in copies:
         one.wait()
+    inner_out[...] = jnp.concatenate(split3(inner[...]), axis=0)
 
 
 def pack_kernel(mine, theirs, out):
@@ -105,7 +106,7 @@
     field,
     diag,
     face,
-    x_inner,
+    from_core,
     x_outer,
     y_halo,
     placed,
@@ -122,12 +123,20 @@
     y_at = lax.broadcasted_iota(jnp.int32, (cells_y, cells_z), 0)
     first_z, last_z = z_at == 0, z_at == cells_z - 1
     first_y, last_y = y_at == 0, y_at == cells_y - 1
+    faces = 2 * cells_y
+    first_term = from_core.shape[0] - 3 * faces
+    terms = [
+        from_core[first_term + term * faces : first_term + (term + 1) * faces, :]
+        for term in range(3)
+    ]
+    terms = [term.astype(jnp.float32) for term in terms]
+    near_rows = (terms[0] + terms[1]) + terms[2]
     stores = []
     for x in range(cells_x):
         own = [field[c, x] for c in range(3)]
         x_plus, x_minus = {}, {}
         for slot, comp in enumerate((1, 2)):
-            near = x_inner[slot * cells_y : (slot + 1) * cells_y, :]
+            near = near_rows[slot * cells_y : (slot + 1) * cells_y, :]
             far = x_outer[slot * cells_y : (slot + 1) * cells_y, :]
             if x + 1 < cells_x:
                 x_plus[comp] = field[comp, x + 1]
@@ -185,14 +194,26 @@
 
 
 def integral_kernel(
-    steps, x_index, y_index, mine, theirs, right, left, own_out, send_out, stack, partial_value
+    steps,
+    x_index,
+    y_index,
+    held,
+    got,
+    cross,
+    from_core,
+    right,
+    left,
+    own_out,
+    send_out,
+    stack,
+    partial_value,
 ):
     columns = left.shape[1]
     rank, groups, count = right.shape
     pitch = count // LANES
-    held = mine.shape[0]
-    stack[0:held, :] = mine[...].astype(jnp.float32)
-    stack[held:, :] = theirs[...].astype(jnp.float32)
+    size = held.shape[0]
+    for i, piece in enumerate((held, got, cross, from_core)):
+        stack[i * size : (i + 1) * size, :] = piece[0:size, :].astype(jnp.float32)
     pieces = [stack[pl.ds(q, groups, stride=pitch), :] for q in range(pitch)]
     gathered = jnp.concatenate(pieces, axis=1).astype(jnp.bfloat16)
     table = right[...].reshape(rank * groups, count)
@@ -202,6 +223,11 @@
     source = jnp.full((rank, groups, groups), x_index[0], jnp.int32)
     for bit, step in enumerate(steps):
         source = source ^ (((block >> bit) & 1) * step)
+    piece = block >> len(steps)
+    mask = jnp.where(x_index[0] % 2 == 0, 2, 4)
+    source = source ^ jnp.where(piece == 1, mask, 0)
+    source = source ^ jnp.where(piece == 2, 6, 0)
+    source = source ^ jnp.where(piece == 3, (6 - mask) ^ 1, 0)
     group = lax.broadcasted_iota(jnp.int32, (rank, groups, groups), 1)
     product = jnp.where(source == group, product, 0.0)
     coef = jnp.sum(jnp.sum(product, axis=1, keepdims=True), axis=2, keepdims=True)
@@ -268,42 +294,49 @@
         up = [(i, i + 1) for i in range(1, size - 1, 2)]
         return up + [(j, i) for i, j in up]
 
-    core_got = lax.ppermute(boundary, "gx", inner_pairs(n_x))
+    def xor_pairs(step, odd_step=None):
+        return [(i, i ^ (odd_step if odd_step and i % 2 else step)) for i in range(n_x)]
+
+    got = lax.ppermute(boundary, "gx", xor_pairs(1))
     inner_pay, outer_pay, y_pay, near_boundary = call(
         halo_kernel,
         [
-            pltpu.VMEM((2 * cells_y, LANES), f32),
+            pltpu.VMEM((3 * 2 * cells_y, LANES), jnp.bfloat16),
             pltpu.VMEM((2 * cells_y, LANES), f32),
             pltpu.VMEM((y_sides, 2 * cells_x, LANES), f32),
             pltpu.VMEM(row, f32),
         ],
         [volume_field, boundary],
-        [pltpu.SemaphoreType.DMA((5 + 2 * y_sides,))],
+        [
+            pltpu.VMEM((2 * cells_y, LANES), f32),
+            pltpu.SemaphoreType.DMA((5 + 2 * y_sides,)),
+        ],
         far=2,
         cost=COST,
     )
-    x_inner = lax.ppermute(inner_pay, "gx", inner_pairs(n_x))
     x_outer = lax.ppermute(outer_pay, "gx", outer_pairs(n_x))
     y_halo = lax.ppermute(y_pay[0], "gy", inner_pairs(n_y))[None]
     if y_sides == 2:
         y_far = lax.ppermute(y_pay[1], "gy", outer_pairs(n_y))[None]
         y_halo = jnp.concatenate([y_halo, y_far], axis=0)
-
-    (mine,) = call(
+    (held,) = call(
         pack_kernel,
         [pltpu.VMEM((2 * rows, LANES), jnp.bfloat16)],
-        [near_boundary, core_got],
+        [near_boundary, got],
         indices=False,
     )
     steps = [1]
-    step = 2
-    while step < n_x:
+    step = n_x // 2
+    while step > 4:
         steps.append(step)
-        pairs = [(i, i ^ step) for i in range(n_x)]
-        theirs = lax.ppermute(mine, "gx", pairs)
-        if 2 * step < n_x:
-            mine = jnp.concatenate([mine, theirs], axis=0)
-        step *= 2
+        got = lax.ppermute(held, "gx", xor_pairs(step))
+        held = jnp.concatenate([held, got], axis=0)
+        step //= 2
+    cross = lax.ppermute(held, "gx", xor_pairs(6))
+    got = lax.ppermute(held, "gx", xor_pairs(2, 4))
+    from_core = lax.ppermute(
+        jnp.concatenate([got, inner_pay], axis=0), "gx", xor_pairs(1)
+    )
 
     placed, base = call(
         prepare_kernel,
@@ -323,8 +356,10 @@
         functools.partial(integral_kernel, tuple(steps)),
         [pltpu.VMEM(row, f32), pltpu.VMEM((n_y - 1, 1, count), f32)],
         [
-            mine,
-            theirs,
+            held,
+            got,
+            cross,
+            from_core,
             right_basis.reshape(rank, n_x, count),
             left_basis.reshape(rank, n_y, count),
         ],
@@ -338,7 +373,7 @@
     (volume_out,) = call(
         stencil_kernel,
         [jax.ShapeDtypeStruct(volume_field.shape, f32)],
-        [volume_field, diag_blocks, face_weights, x_inner, x_outer, y_halo, placed],
+        [volume_field, diag_blocks, face_weights, from_core, x_outer, y_halo, placed],
         [pltpu.VMEM(volume_field.shape, f32), pltpu.SemaphoreType.DMA((4,))],
         far_outs=1,
         cost=COST,

time: 22 us -> 22.9 us (1.041)
  starting transfers between devices: 12.6 us -> 14 us
  waiting for transfers between devices: 3.94 us -> 2.98 us
  local copies, waits for them, and re-layouts: 0.74 us -> 1.03 us
    ppermute x5, starting transfers between devices: 9.75 us -> 11.2 us  [the longest x1 3.98 us: on_device(): got = lax.ppermute(held, 'gx', xor_pairs(step))]
    ppermute x5, waiting for transfers between devices: 2.82 us -> 1.85 us  [the longest x1 1.61 us: on_device(): got = lax.ppermute(held, 'gx', xor_pairs(step))]
    unnamed x16, local copies, waits for them, and re-layouts: 0.74 us -> 1.03 us
where the time goes in v4:
time: 22.9 us; the launch traced here: 22.7 us
  starting transfers between devices  14 us (61%)
  Pallas kernels  3.31 us (14%)
  waiting for transfers between devices  2.98 us (13%)
  local copies, waits for them, and re-layouts  1.03 us (4%)
  between operations  0.71 us (3%)
  other arithmetic  0.61 us (3%)
    ppermute x1, starting transfers between devices, on_device(): got = lax.ppermute(held, 'gx', xor_pairs(step))  3.98 us
    pallas_call x5, Pallas kernels, call(): pl.pallas_call(body, out_shape=outs, in_specs=[smem] * len(lead) + [hbm]...  3.31 us
    ppermute x1, starting transfers between devices, on_device(): cross = lax.ppermute(held, 'gx', xor_pairs(6))  2.81 us
    ppermute x1, starting transfers between devices, on_device(): lax.ppermute(jnp.concatenate([got, inner_pay], axis=0), 'gx', xor_pairs(1))  2.05 us
    ppermute x1, starting transfers between devices, on_device(): got = lax.ppermute(held, 'gx', xor_pairs(2, 4))  1.82 us
    ppermute x1, waiting for transfers between devices, on_device(): got = lax.ppermute(held, 'gx', xor_pairs(step))  1.61 us
    ppermute x1, starting transfers between devices, on_device(): y_halo = lax.ppermute(y_pay[0], 'gy', inner_pairs(n_y))[None]  1.58 us
    ppermute x1, waiting for transfers between devices, on_device(): total = total + lax.ppermute(shares[shift - 1], 'gy', pairs)  1.12 us
  transfers between devices with their start and end apart: 8, of which 4 were waited for; matrix products, arithmetic and copies ran while one was open for 0% of the time, Pallas kernels for 15%

profile of v4, /device:TPU:0, one launch (start us, length us, event | category | flops | bytes accessed | tf_op | source)
XLA Modules:
  0.0 22.7 jit_solution(11489712035907169434)
XLA Ops:
  0.6 0.6 %collective-permute-start = (f32[1,1536]{1,0:T(1,128)}, f32[1,1536]{1,0:T(1,128)S(1)}, u32[]{:S(2)}, u32[]{:S(2)}) collective-permute-start(f32[1,1536]{1,0:T(1,128)} %bitcast.21), channel_id=1, source_target_pairs={{0,2},{2,0},{4,6},{6,4},{8,10},{10,8},{12,14},{14,12},{16,18},{18,... | collective-permute-start | bytes 18440 | tf_op jit(solution)/shard_map/ppermute | solution.py:300
  1.2 0.0 copy-start.3
  1.2 0.0 copy-start.5
  1.2 0.0 copy-start.6
  1.2 0.0 copy-start.7
  1.2 0.9 %shard_map.104 = (bf16[96,128]{1,0:T(8,128)(2,1)S(1)}, f32[32,128]{1,0:T(8,128)S(1)}, f32[1,32,128]{2,1,0:T(8,128)S(1)}, f32[1,1536]{1,0:T(1,128)S(1)}) custom-call(s32[1]{0:T(128)} %bitcast.x_index, s32[1]{0:T(128)} %bitcast.1.y_index, f32[3,16,16,128]{3,2,1,0:T(8,128)} %field.5, f32[1,1536]{1,0:T(1,128)} %bitcast.22), custom_call_target="tpu_custom_call" | custom-call | flops 10000000000 | tf_op jit(solution)/shard_map/pallas_call | solution.py:280
  2.1 0.1 collective-permute-done.theirs
  2.2 4.0 %collective-permute-start.1 = (bf16[24,128]{1,0:T(8,128)(2,1)S(1)}, bf16[24,128]{1,0:T(8,128)(2,1)S(1)}, u32[]{:S(2)}, u32[]{:S(2)}) collective-permute-start(bf16[24,128]{1,0:T(8,128)(2,1)S(1)} %shard_map.105), channel_id=1, source_target_pairs={{0,16},{2,18},{4,20},{6,22},{8,24},{10,26},{12,28},{14,30},{16,0},... | collective-permute-start | bytes 18440 | tf_op jit(solution)/shard_map/ppermute | solution.py:332
  6.2 1.6 %collective-permute-done.1 = bf16[24,128]{1,0:T(8,128)(2,1)S(1)} collective-permute-done((bf16[24,128]{1,0:T(8,128)(2,1)S(1)}, bf16[24,128]{1,0:T(8,128)(2,1)S(1)}, u32[]{:S(2)}, u32[]{:S(2)}) %collective-permute-start.1) | collective-permute-done | bytes 6176 | tf_op jit(solution)/shard_map/ppermute | solution.py:332
  7.8 1.8 %collective-permute-start.2 = (bf16[48,128]{1,0:T(8,128)(2,1)S(1)}, bf16[48,128]{1,0:T(8,128)(2,1)S(1)}, u32[]{:S(2)}, u32[]{:S(2)}) collective-permute-start(bf16[48,128]{1,0:T(8,128)(2,1)S(1)} %pad_maximum_fusion.1.held), channel_id=1, source_target_pairs={{0,4},{2,10},{4,0},{6,14},{8,12},{10,2},{12,8},{14,6},{16,20},{18,... | collective-permute-start | bytes 36872 | tf_op jit(solution)/shard_map/ppermute | solution.py:336
  9.7 0.7 %collective-permute-start.4 = (f32[32,128]{1,0:T(8,128)S(1)}, f32[32,128]{1,0:T(8,128)S(1)}, u32[]{:S(2)}, u32[]{:S(2)}) collective-permute-start(f32[32,128]{1,0:T(8,128)S(1)} %get-tuple-element.12), channel_id=1, source_target_pairs={{2,4},{6,8},{10,12},{14,16},{18,20},{22,24},{26,28},{4,2},{8,6},{1... | collective-permute-start | bytes 49160 | tf_op jit(solution)/shard_map/ppermute | solution.py:317
  10.3 1.6 %collective-permute-start.5 = (f32[32,128]{1,0:T(8,128)S(1)}, f32[32,128]{1,0:T(8,128)S(1)}, u32[]{:S(2)}, u32[]{:S(2)}) collective-permute-start(f32[32,128]{1,0:T(8,128)S(1)} %bitcast.15), channel_id=1, source_target_pairs={{0,1},{1,0},{2,3},{3,2},{4,5},{5,4},{6,7},{7,6},{8,9},{9,8},{10,11... | collective-permute-start | bytes 49160 | tf_op jit(solution)/shard_map/ppermute | solution.py:318
  11.9 2.8 %collective-permute-start.6 = (bf16[48,128]{1,0:T(8,128)(2,1)S(1)}, bf16[48,128]{1,0:T(8,128)(2,1)S(1)}, u32[]{:S(2)}, u32[]{:S(2)}) collective-permute-start(bf16[48,128]{1,0:T(8,128)(2,1)S(1)} %pad_maximum_fusion.1.held), channel_id=1, source_target_pairs={{0,12},{2,14},{4,8},{6,10},{8,4},{10,6},{12,0},{14,2},{16,28},{18,... | collective-permute-start | bytes 36872 | tf_op jit(solution)/shard_map/ppermute | solution.py:335
  14.7 0.0 collective-permute-done.2.got
  14.7 2.0 %collective-permute-start.3 = (bf16[144,128]{1,0:T(8,128)(2,1)S(1)}, bf16[144,128]{1,0:T(8,128)(2,1)S(1)}, u32[]{:S(2)}, u32[]{:S(2)}) collective-permute-start(bf16[144,128]{1,0:T(8,128)(2,1)S(1)} %pad_maximum_fusion), channel_id=1, source_target_pairs={{0,2},{2,0},{4,6},{6,4},{8,10},{10,8},{12,14},{14,12},{16,18},{18,... | collective-permute-start | bytes 110600 | tf_op jit(solution)/shard_map/ppermute | solution.py:337
  16.8 0.0 copy-done.3
  16.8 0.0 copy-done.5
  16.8 0.0 copy-done.6
  16.8 0.0 copy-done.7
  16.8 0.0 copy-start.2
  16.8 0.0 copy-start.4
  16.8 0.7 %shard_map.106 = (f32[128,16]{1,0:T(8,128)S(1)}, f32[1,1536]{1,0:T(1,128)S(1)}) custom-call(f32[3,16,16,128]{3,2,1,0:T(8,128)S(1)} %copy-done.3, f32[1,1536]{1,0:T(1,128)S(1)} %get-tuple-element.10.mine.boundary, f32[1,1536]{1,0:T(1,128)S(1)} %bitcast.17, f32[1,1536]{1,0:T(1,128)S(1)} %bitcast.18, s32[1,1536]{1,0:T(1,128)S(1)} %bitcast.19), custom_call_target="tpu_custom_call" | custom-call | flops 10000000000 | tf_op jit(solution)/shard_map/pallas_call | solution.py:280
  17.5 0.0 collective-permute-done.6.cross
  17.5 0.1 collective-permute-done.3.from_core
  17.6 0.3 %copy-done.2 = bf16[16,16,1,1536]{3,1,2,0:T(8,128)(2,1)S(1)} copy-done((bf16[16,16,1,1536]{3,1,2,0:T(8,128)(2,1)S(1)}, bf16[16,16,1,1536]{3,1,2,0:T(8,128)(2,1)}, u32[]{:S(2)}) %copy-start.2) | copy-done | bytes 786456
  17.9 0.0 copy-done.4
  17.9 0.0 copy-start
  17.9 0.0 copy-start.1
  17.9 0.4 %shard_map.108 = (f32[1,1536]{1,0:T(1,128)S(1)}, f32[1,1,1536]{2,1,0:T(1,128)S(1)}) custom-call(s32[1]{0:T(128)} %bitcast.x_index, s32[1]{0:T(128)} %bitcast.1.y_index, bf16[48,128]{1,0:T(8,128)(2,1)S(1)} %pad_maximum_fusion.1.held, bf16[48,128]{1,0:T(8,128)(2,1)S(1)} %collective-permute-done.2.got, bf16[48,128]{1,0:T(8,128)(2,1)S(1)} %collective-permute-done.6.cross, ...), custom_call_target="tpu_custom_call" | custom-call | flops 10000000000 | tf_op jit(solution)/shard_map/pallas_call | solution.py:280
  18.4 0.6 %collective-permute-start.7 = (f32[1,1536]{1,0:T(1,128)S(1)}, f32[1,1536]{1,0:T(1,128)S(1)}, u32[]{:S(2)}, u32[]{:S(2)}) collective-permute-start(f32[1,1536]{1,0:T(1,128)S(1)} %bitcast.20), channel_id=1, source_target_pairs={{0,1},{1,0},{2,3},{3,2},{4,5},{5,4},{6,7},{7,6},{8,9},{9,8},{10,11... | collective-permute-start | bytes 18440 | tf_op jit(solution)/shard_map/ppermute | solution.py:384
  18.9 0.0 collective-permute-done.4.x_outer
  18.9 0.0 collective-permute-done.5
  18.9 0.4 %copy-done = f32[6,2,16,16,128]{4,3,2,1,0:T(8,128)S(1)} copy-done((f32[6,2,16,16,128]{4,3,2,1,0:T(8,128)S(1)}, f32[6,2,16,16,128]{4,3,2,1,0:T(8,128)}, u32[]{:S(2)}) %copy-start) | copy-done | bytes 1572888
  19.3 0.3 %copy-done.1 = f32[3,3,16,16,128]{4,3,2,1,0:T(8,128)S(1)} copy-done((f32[3,3,16,16,128]{4,3,2,1,0:T(8,128)S(1)}, f32[3,3,16,16,128]{4,3,2,1,0:T(8,128)}, u32[]{:S(2)}) %copy-start.1) | copy-done | bytes 1179672
  19.7 1.3 %shard_map.107 = f32[3,16,16,128]{3,2,1,0:T(8,128)} custom-call(s32[1]{0:T(128)} %bitcast.x_index, s32[1]{0:T(128)} %bitcast.1.y_index, f32[3,16,16,128]{3,2,1,0:T(8,128)S(1)} %copy-done.3, f32[3,3,16,16,128]{4,3,2,1,0:T(8,128)S(1)} %copy-done.1, f32[6,2,16,16,128]{4,3,2,1,0:T(8,128)S(1)} %copy-done, bf16[144,128]{1,0:T(8,128)(2,1)S(1)} %collective-permute-done.3.from_core, ...), custom_call_target="tpu_custom_call" | custom-call | flops 10000000000 | tf_op jit(solution)/shard_map/pallas_call | solution.py:280
  20.9 1.1 %collective-permute-done.7 = f32[1,1536]{1,0:T(1,128)S(1)} collective-permute-done((f32[1,1536]{1,0:T(1,128)S(1)}, f32[1,1536]{1,0:T(1,128)S(1)}, u32[]{:S(2)}, u32[]{:S(2)}) %collective-permute-start.7) | collective-permute-done | bytes 6176 | tf_op jit(solution)/shard_map/ppermute | solution.py:384
  22.1 0.6 %add_bitcast_fusion = f32[1,1,1536]{2,1,0:T(1,128)} fusion(f32[1,1536]{1,0:T(1,128)S(1)} %collective-permute-done.7, f32[1,1536]{1,0:T(1,128)S(1)} %get-tuple-element.15, f32[1,1536]{1,0:T(1,128)S(1)} %get-tuple-element.16), kind=kLoop, calls=%fused_computation.2 | loop fusion | flops 3072 | bytes 24576 | tf_op jit(solution)/shard_map/reshape | solution.py:385
  (3 shorter events, 0.0 us)
Async XLA Ops:
  0.6 1.6 %collective-permute-start = (f32[1,1536]{1,0:T(1,128)}, f32[1,1536]{1,0:T(1,128)S(1)}, u32[]{:S(2)}, u32[]{:S(2)}) collective-permute-start(f32[1,1536]{1,0:T(1,128)} %bitcast.21), channel_id=1, source_target_pairs={{0,2},{2,0},{4,6},{6,4},{8,10},{10,8},{12,14},{14,12},{16,18},{18,... | collective-permute-start | bytes 18440 | tf_op jit(solution)/shard_map/ppermute | solution.py:300
  1.2 15.6 %copy-start.3 = (f32[3,16,16,128]{3,2,1,0:T(8,128)S(1)}, f32[3,16,16,128]{3,2,1,0:T(8,128)}, u32[]{:S(2)}) copy-start(f32[3,16,16,128]{3,2,1,0:T(8,128)} %field.5) | copy-start | bytes 1179652
  1.2 15.6 %copy-start.5 = (f32[1,1,1536]{2,1,0:T(1,128)S(1)}, f32[1,1,1536]{2,1,0:T(1,128)}, u32[]{:S(2)}) copy-start(f32[1,1,1536]{2,1,0:T(1,128)} %param.13) | copy-start | bytes 18436
  1.2 15.6 %copy-start.6 = (f32[1,1,1536]{2,1,0:T(1,128)S(1)}, f32[1,1,1536]{2,1,0:T(1,128)}, u32[]{:S(2)}) copy-start(f32[1,1,1536]{2,1,0:T(1,128)} %param.14) | copy-start | bytes 18436
  1.2 15.6 %copy-start.7 = (s32[1,1,1536]{2,1,0:T(1,128)S(1)}, s32[1,1,1536]{2,1,0:T(1,128)}, u32[]{:S(2)}) copy-start(s32[1,1,1536]{2,1,0:T(1,128)} %param.15) | copy-start | bytes 18436
  2.2 5.6 %collective-permute-start.1 = (bf16[24,128]{1,0:T(8,128)(2,1)S(1)}, bf16[24,128]{1,0:T(8,128)(2,1)S(1)}, u32[]{:S(2)}, u32[]{:S(2)}) collective-permute-start(bf16[24,128]{1,0:T(8,128)(2,1)S(1)} %shard_map.105), channel_id=1, source_target_pairs={{0,16},{2,18},{4,20},{6,22},{8,24},{10,26},{12,28},{14,30},{16,0},... | collective-permute-start | bytes 18440 | tf_op jit(solution)/shard_map/ppermute | solution.py:332
  7.8 6.9 %collective-permute-start.2 = (bf16[48,128]{1,0:T(8,128)(2,1)S(1)}, bf16[48,128]{1,0:T(8,128)(2,1)S(1)}, u32[]{:S(2)}, u32[]{:S(2)}) collective-permute-start(bf16[48,128]{1,0:T(8,128)(2,1)S(1)} %pad_maximum_fusion.1.held), channel_id=1, source_target_pairs={{0,4},{2,10},{4,0},{6,14},{8,12},{10,2},{12,8},{14,6},{16,20},{18,... | collective-permute-start | bytes 36872 | tf_op jit(solution)/shard_map/ppermute | solution.py:336
  9.7 9.3 %collective-permute-start.4 = (f32[32,128]{1,0:T(8,128)S(1)}, f32[32,128]{1,0:T(8,128)S(1)}, u32[]{:S(2)}, u32[]{:S(2)}) collective-permute-start(f32[32,128]{1,0:T(8,128)S(1)} %get-tuple-element.12), channel_id=1, source_target_pairs={{2,4},{6,8},{10,12},{14,16},{18,20},{22,24},{26,28},{4,2},{8,6},{1... | collective-permute-start | bytes 49160 | tf_op jit(solution)/shard_map/ppermute | solution.py:317
  10.3 8.6 %collective-permute-start.5 = (f32[32,128]{1,0:T(8,128)S(1)}, f32[32,128]{1,0:T(8,128)S(1)}, u32[]{:S(2)}, u32[]{:S(2)}) collective-permute-start(f32[32,128]{1,0:T(8,128)S(1)} %bitcast.15), channel_id=1, source_target_pairs={{0,1},{1,0},{2,3},{3,2},{4,5},{5,4},{6,7},{7,6},{8,9},{9,8},{10,11... | collective-permute-start | bytes 49160 | tf_op jit(solution)/shard_map/ppermute | solution.py:318
  11.9 5.6 %collective-permute-start.6 = (bf16[48,128]{1,0:T(8,128)(2,1)S(1)}, bf16[48,128]{1,0:T(8,128)(2,1)S(1)}, u32[]{:S(2)}, u32[]{:S(2)}) collective-permute-start(bf16[48,128]{1,0:T(8,128)(2,1)S(1)} %pad_maximum_fusion.1.held), channel_id=1, source_target_pairs={{0,12},{2,14},{4,8},{6,10},{8,4},{10,6},{12,0},{14,2},{16,28},{18,... | collective-permute-start | bytes 36872 | tf_op jit(solution)/shard_map/ppermute | solution.py:335
  14.7 2.9 %collective-permute-start.3 = (bf16[144,128]{1,0:T(8,128)(2,1)S(1)}, bf16[144,128]{1,0:T(8,128)(2,1)S(1)}, u32[]{:S(2)}, u32[]{:S(2)}) collective-permute-start(bf16[144,128]{1,0:T(8,128)(2,1)S(1)} %pad_maximum_fusion), channel_id=1, source_target_pairs={{0,2},{2,0},{4,6},{6,4},{8,10},{10,8},{12,14},{14,12},{16,18},{18,... | collective-permute-start | bytes 110600 | tf_op jit(solution)/shard_map/ppermute | solution.py:337
  16.8 1.1 %copy-start.2 = (bf16[16,16,1,1536]{3,1,2,0:T(8,128)(2,1)S(1)}, bf16[16,16,1,1536]{3,1,2,0:T(8,128)(2,1)}, u32[]{:S(2)}) copy-start(bf16[16,16,1,1536]{3,1,2,0:T(8,128)(2,1)} %param.17) | copy-start | bytes 2359300
  16.8 1.1 %copy-start.4 = (bf16[16,1,2,1536]{3,2,1,0:T(2,128)(2,1)S(1)}, bf16[16,1,2,1536]{3,2,1,0:T(2,128)(2,1)}, u32[]{:S(2)}) copy-start(bf16[16,1,2,1536]{3,2,1,0:T(2,128)(2,1)} %param.16) | copy-start | bytes 294916
  17.9 1.4 %copy-start = (f32[6,2,16,16,128]{4,3,2,1,0:T(8,128)S(1)}, f32[6,2,16,16,128]{4,3,2,1,0:T(8,128)}, u32[]{:S(2)}) copy-start(f32[6,2,16,16,128]{4,3,2,1,0:T(8,128)} %face.1) | copy-start | bytes 4718596
  17.9 1.7 %copy-start.1 = (f32[3,3,16,16,128]{4,3,2,1,0:T(8,128)S(1)}, f32[3,3,16,16,128]{4,3,2,1,0:T(8,128)}, u32[]{:S(2)}) copy-start(f32[3,3,16,16,128]{4,3,2,1,0:T(8,128)} %diag.1) | copy-start | bytes 3538948
  18.4 3.7 %collective-permute-start.7 = (f32[1,1536]{1,0:T(1,128)S(1)}, f32[1,1536]{1,0:T(1,128)S(1)}, u32[]{:S(2)}, u32[]{:S(2)}) collective-permute-start(f32[1,1536]{1,0:T(1,128)S(1)} %bitcast.20), channel_id=1, source_target_pairs={{0,1},{1,0},{2,3},{3,2},{4,5},{5,4},{6,7},{7,6},{8,9},{9,8},{10,11... | collective-permute-start | bytes 18440 | tf_op jit(solution)/shard_map/ppermute | solution.py:384
